TPU v7x, 128 devices: a whole 4x4x4 slice. The times are simulated.
128 devices in a mesh: enc: 8 (over z, core), gen: 16 (over x, y).
Axes of the slice: x: 4, y: 4, z: 4, core: 2. Of those that a mesh axis runs over, the one named last changes fastest.
Arguments:
- hidden_states: bfloat16 [8192, 4096], P('gen'), may hold values from -60 to 60
- grad_out: bfloat16 [8192, 4096], P('gen'), may hold values from -0.29882812 to 0.29882812
- nbr_embed: bfloat16 [256, 128, 1024], P(('enc', 'gen')), may hold values from -60 to 60
- nbr_index: int32 [128, 2], replicated, may hold values from 0 to 255, as said below
- gain: float32 [4096], replicated, may hold values from 0.5 to 1.5
- w_query: bfloat16 [4096, 4096], P(None, 'enc'), may hold values from -0.1875 to 0.1875
- w_out: bfloat16 [4096, 4096], P('enc'), may hold values from -0.09375 to 0.09375
- w_key: bfloat16 [1024, 4096], P(None, 'enc'), may hold values from -0.1875 to 0.1875
- w_value: bfloat16 [1024, 4096], P(None, 'enc'), may hold values from -0.75 to 0.75
- enc_gain: float32 [1024], replicated, may hold values from 0.5 to 1.5
- enc_qkv: bfloat16 [1024, 3072], replicated, may hold values from -0.1875 to 0.1875
- enc_out: bfloat16 [1024, 1024], replicated, may hold values from -0.1875 to 0.1875
Outputs:
- grad_encoded: float32 [256, 128, 1024], P(('enc', 'gen'))
- grad_w_out: float32 [4096, 4096], P('enc', 'gen')
- grad_w_key: float32 [1024, 4096], P('gen', 'enc')
- grad_w_value: float32 [1024, 4096], P('gen', 'enc')
Inputs may be any that keep to these rules, and one draw needn't show every extreme that they name: `nbr_index`: every entry 0 to 255 is named exactly once. Entry p is held by index (p // 2) % 16 of gen; block c belongs to index c * 64 // 512 of gen. The blocks of one index of gen name at most 2 entries held by one index of gen, and some pair of indices reaches 2 in every draw.
All inputs are finite; a program needn't handle non-finite values.
Results may differ from a plain program's by a relative error of at most 0.038.
Values may be sent and summed in bfloat16 or wider, within the bound.
A program may use at most 128 MiB of HBM per device.

v0:
```python
import jax
import jax.numpy as jnp
from jax import lax
from jax.sharding import PartitionSpec as P

H = 32
EH = 8
CH = 64
K = 2


SOFTCAP = 5.0
EPSILON = 1e-06


def rms_scale(values, gain):
    wide = values.astype(jnp.float32)
    factor = lax.rsqrt(jnp.mean(wide * wide, axis=-1, keepdims=True) + EPSILON)
    return (wide * factor * gain).astype(jnp.bfloat16)


def attention_parts(queries, keys_all, values_all):
    head_width = queries.shape[-1]
    raw_scores = jnp.einsum(
        "bqhd,bkhd->bhqk", queries, keys_all, preferred_element_type=jnp.float32
    ) * head_width ** (-0.5)
    capped = SOFTCAP * jnp.tanh(raw_scores / SOFTCAP)
    expo_terms = jnp.exp(capped)
    probs_full = expo_terms / jnp.sum(expo_terms, axis=-1, keepdims=True)
    probs_low = probs_full.astype(jnp.bfloat16)
    mixed = jnp.einsum(
        "bhqk,bkhd->bqhd", probs_low, values_all, preferred_element_type=jnp.float32
    ).astype(jnp.bfloat16)
    return (raw_scores, probs_full, probs_low, mixed)


def attention_grads(queries, values_all, raw_scores, probs_full, probs_low, d_mixed):
    head_width = queries.shape[-1]
    d_probs = jnp.einsum("bqhd,bkhd->bhqk", d_mixed, values_all, preferred_element_type=jnp.float32)
    d_capped = probs_full * (d_probs - jnp.sum(probs_full * d_probs, axis=-1, keepdims=True))
    slope = jnp.tanh(raw_scores / SOFTCAP)
    d_raw = (d_capped * (1.0 - slope * slope) * head_width ** (-0.5)).astype(jnp.bfloat16)
    d_keys = jnp.einsum(
        "bhqk,bqhd->bkhd", d_raw, queries, preferred_element_type=jnp.float32
    ).astype(jnp.bfloat16)
    d_values = jnp.einsum(
        "bhqk,bqhd->bkhd", probs_low, d_mixed, preferred_element_type=jnp.float32
    ).astype(jnp.bfloat16)
    return (d_keys, d_values)


def encode(nbr_embed, enc_gain, enc_qkv, enc_out):
    entries, length, enc_width = nbr_embed.shape
    normed = rms_scale(nbr_embed, enc_gain).reshape(entries * length, enc_width)
    projected = jnp.dot(normed, enc_qkv, preferred_element_type=jnp.float32).astype(jnp.bfloat16)
    projected = projected.reshape(entries, length, 3, EH, enc_width // EH)
    outputs = attention_parts(projected[:, :, 0], projected[:, :, 1], projected[:, :, 2])
    attended = outputs[3].reshape(entries * length, enc_width)
    update = jnp.dot(attended, enc_out, preferred_element_type=jnp.float32).reshape(
        entries, length, enc_width
    )
    return (nbr_embed.astype(jnp.float32) + update).astype(jnp.bfloat16)


def routing(nbr_index, row_index, gen_count, per_device, row_size, capacity):
    slot_entries = nbr_index.reshape(-1)
    entry_count = slot_entries.shape[0]
    slot_ids = jnp.arange(entry_count, dtype=jnp.int32)
    target = slot_ids // row_size
    source = slot_entries // per_device % gen_count
    column = slot_entries // (per_device * gen_count) * per_device + slot_entries % per_device
    pair_ids = target * gen_count + source
    pair_onehot = (
        pair_ids[:, None] == jnp.arange(gen_count * gen_count, dtype=jnp.int32)[None, :]
    ).astype(jnp.int32)
    earlier = jnp.cumsum(pair_onehot, axis=0) - pair_onehot
    rank_in = jnp.sum(earlier * pair_onehot, axis=1)
    send_slot = target * capacity + rank_in
    buffer_ids = jnp.arange(gen_count * capacity, dtype=jnp.int32)
    is_mine = (source == row_index).astype(jnp.int32)
    send_match = (send_slot[:, None] == buffer_ids[None, :]).astype(jnp.int32) * is_mine[:, None]
    send_column = jnp.sum(send_match * column[:, None], axis=0)
    column_ids = jnp.arange(row_size, dtype=jnp.int32)
    column_match = (column[:, None] == column_ids[None, :]).astype(jnp.int32) * is_mine[:, None]
    column_position = jnp.sum(column_match * send_slot[:, None], axis=0)
    own_source = lax.dynamic_slice_in_dim(source, row_index * row_size, row_size)
    own_rank = lax.dynamic_slice_in_dim(rank_in, row_index * row_size, row_size)
    receive_position = own_source * capacity + own_rank
    receive_match = (receive_position[:, None] == buffer_ids[None, :]).astype(jnp.int32)
    position_slot = jnp.sum(receive_match * column_ids[:, None], axis=0)
    return (send_column, column_position, receive_position, position_slot)


def local(
    hidden_states,
    grad_out,
    nbr_embed,
    nbr_index,
    gain,
    w_query,
    w_out,
    w_key,
    w_value,
    enc_gain,
    enc_qkv,
    enc_out,
):
    enc_count = lax.axis_size("enc")
    gen_count = lax.axis_size("gen")
    row_index = lax.axis_index("gen")
    per_device, length, enc_width = nbr_embed.shape
    row_size = per_device * enc_count
    capacity = max(2, 2 * row_size // gen_count)
    token_count, model_width = hidden_states.shape
    head_feats = w_query.shape[1]
    head_width = model_width // H
    head_count = head_feats // head_width
    block_count = token_count // CH
    send_column, column_position, receive_position, position_slot = routing(
        nbr_index, row_index, gen_count, per_device, row_size, capacity
    )
    encoded = encode(nbr_embed, enc_gain, enc_qkv, enc_out)
    row_encoded = lax.all_gather(encoded, "enc", axis=0, tiled=True)
    outgoing = jnp.take(row_encoded, send_column, axis=0)
    incoming = lax.all_to_all(outgoing, "gen", split_axis=0, concat_axis=0, tiled=True)
    slot_encoded = jnp.take(incoming, receive_position, axis=0)
    slot_rows = slot_encoded.reshape(row_size * length, enc_width)
    normed = rms_scale(hidden_states, gain)
    queries = jnp.dot(normed, w_query, preferred_element_type=jnp.float32).astype(jnp.bfloat16)
    queries = queries.reshape(block_count, CH, head_count, head_width)
    keys_all = jnp.dot(slot_rows, w_key, preferred_element_type=jnp.float32).astype(jnp.bfloat16)
    values_all = jnp.dot(slot_rows, w_value, preferred_element_type=jnp.float32).astype(
        jnp.bfloat16
    )
    keys_all = keys_all.reshape(block_count, K * length, head_count, head_width)
    values_all = values_all.reshape(block_count, K * length, head_count, head_width)
    raw_scores, probs_full, probs_low, mixed = attention_parts(queries, keys_all, values_all)
    mixed_rows = mixed.reshape(token_count, head_feats)
    d_mixed = jnp.dot(grad_out, w_out.T, preferred_element_type=jnp.float32).astype(jnp.bfloat16)
    out_term = jnp.dot(mixed_rows.T, grad_out, preferred_element_type=jnp.float32)
    d_keys, d_values = attention_grads(
        queries,
        values_all,
        raw_scores,
        probs_full,
        probs_low,
        d_mixed.reshape(block_count, CH, head_count, head_width),
    )
    d_keys_rows = d_keys.reshape(row_size * length, head_feats)
    d_values_rows = d_values.reshape(row_size * length, head_feats)
    key_term = jnp.dot(slot_rows.T, d_keys_rows, preferred_element_type=jnp.float32)
    value_term = jnp.dot(slot_rows.T, d_values_rows, preferred_element_type=jnp.float32)
    enc_term = jnp.dot(d_keys_rows, w_key.T, preferred_element_type=jnp.float32) + jnp.dot(
        d_values_rows, w_value.T, preferred_element_type=jnp.float32
    )
    enc_term_low = enc_term.astype(jnp.bfloat16).reshape(row_size, length, enc_width)
    returning = jnp.take(enc_term_low, position_slot, axis=0)
    returned = lax.all_to_all(returning, "gen", split_axis=0, concat_axis=0, tiled=True)
    row_grads = jnp.take(returned, column_position, axis=0).astype(jnp.float32)
    grad_encoded = lax.psum_scatter(
        row_grads.astype(jnp.bfloat16), "enc", scatter_dimension=0, tiled=True
    ).astype(jnp.float32)
    grad_w_out, grad_w_key, grad_w_value = (
        lax.psum_scatter(
            out_term.astype(jnp.bfloat16), "gen", scatter_dimension=1, tiled=True
        ).astype(jnp.float32),
        lax.psum_scatter(
            key_term.astype(jnp.bfloat16), "gen", scatter_dimension=0, tiled=True
        ).astype(jnp.float32),
        lax.psum_scatter(
            value_term.astype(jnp.bfloat16), "gen", scatter_dimension=0, tiled=True
        ).astype(jnp.float32),
    )
    return (grad_encoded, grad_w_out, grad_w_key, grad_w_value)


def solution(mesh):
    return jax.shard_map(
        local,
        mesh=mesh,
        in_specs=(
            P("gen", None),
            P("gen", None),
            P(("enc", "gen"), None, None),
            P(),
            P(),
            P(None, "enc"),
            P("enc", None),
            P(None, "enc"),
            P(None, "enc"),
            P(),
            P(),
            P(),
        ),
        out_specs=(
            P(("enc", "gen"), None, None),
            P("enc", "gen"),
            P("gen", "enc"),
            P("gen", "enc"),
        ),
        check_vma=False,
    )
```

profile of v0, /device:TPU:1, one launch (start us, length us, event | category | flops | bytes accessed | tf_op | source)
XLA Modules:
  0.0 655.1 jit_solution(7774443420112423372)
XLA Ops:
  9.8 4.6 fusion.23
  24.4 34.8 %all-gather.2.cloned.1.call-done = bf16[16,128,1024]{2,1,0:T(8,128)(2,1)} async-done(((bf16[2,128,1024]{2,1,0:T(8,128)(2,1)}), bf16[16,128,1024]{2,1,0:T(8,128)(2,1)}) %all-gather.2.cloned.1.call-update) | async-done | bytes 4194320 | tf_op jit(solution)/shard_map/all_gather | solution.py:123
  59.2 7.1 %gather_fusion = bf16[32,128,1024]{2,1,0:T(8,128)(2,1)} fusion(bf16[16,128,1024]{2,1,0:T(8,128)(2,1)} %all-gather.2.cloned.1.call-done, s32[1024]{0:T(1024)S(1)} %pad_clamp_fusion.3), kind=kCustom, calls=%fused_computation.clone | custom fusion | bytes 16777344 | tf_op jit(solution)/shard_map/jit(_take)/gather | solution.py:124
  66.3 7.5 %broadcast_select_fusion.1 = bf16[32,128,1024]{2,1,0:T(8,128)(2,1)} fusion(bf16[32,128,1024]{2,1,0:T(8,128)(2,1)} %gather_fusion, pred[32]{0:T(512)(128)(4,1)S(1)} %compare_and_fusion.3), kind=kLoop, calls=%fused_computation.12 | loop fusion | flops 4194304 | bytes 16777248 | tf_op jit(solution)/shard_map/jit(_take)/select_n | solution.py:124
  73.7 6.7 %all-to-all-start = ((bf16[32,128,1024]{2,1,0:T(8,128)(2,1)}), bf16[32,128,1024]{2,1,0:T(8,128)(2,1)}, u32[]{:S(2)}, u32[]{:S(2)}) async-start(bf16[32,128,1024]{2,1,0:T(8,128)(2,1)} %broadcast_select_fusion.1), calls=%async_computation | async-start | bytes 16777216 | tf_op jit(solution)/shard_map/all_to_all | solution.py:125
  84.4 4.6 fusion.35
  89.1 5.8 convolution_convert_fusion.6
  95.2 132.4 %all-to-all-done = bf16[32,128,1024]{2,1,0:T(8,128)(2,1)} async-done(((bf16[32,128,1024]{2,1,0:T(8,128)(2,1)}), bf16[32,128,1024]{2,1,0:T(8,128)(2,1)}, u32[]{:S(2)}, u32[]{:S(2)}) %all-to-all-start) | async-done | bytes 8388640 | tf_op jit(solution)/shard_map/all_to_all | solution.py:125
  227.6 6.2 gather_fusion.1
  244.9 6.2 convolution_convert_fusion.3
  251.1 4.0 reshape.224
  259.5 16.0 %convert_bitcast_fusion.1 = bf16[8,256,4,128]{1,3,2,0:T(8,128)(2,1)} fusion(f32[8,4,64,256]{3,2,1,0:T(8,128)} %fusion.19, f32[8,4,64,256]{3,2,1,0:T(8,128)} %get-tuple-element.15, bf16[8,64,4,128]{3,2,1,0:T(4,128)(2,1)S(1)} %reshape.217, f32[8,4,64]{2,1,0:T(4,128)S(1)} %get-tuple-element.14), kind=kOutput, calls=%fused_computation.27 | convolution fusion | flops 142608640 | bytes 6823936 | tf_op jit(solution)/shard_map/bhqk,bqhd->bkhd/dot_general | solution.py:43
  298.4 5.7 fusion.81
  304.1 4.3 convolution_convert_fusion
  308.4 8.5 %add_convert_fusion = bf16[2048,1024]{1,0:T(8,128)(2,1)} fusion(f32[2048,1024]{1,0:T(8,128)} %fusion.81, bf16[2048,512]{0,1:T(8,128)(2,1)} %bitcast.96, bf16[1024,512]{1,0:T(8,128)(2,1)S(1)} %copy-done.15), kind=kOutput, calls=%fused_computation.10 | convolution fusion | flops 2151677952 | bytes 15728640 | tf_op jit(solution)/shard_map/dot_general | solution.py:153
  316.9 7.2 %gather_fusion.2 = bf16[32,128,1024]{2,1,0:T(8,128)(2,1)} fusion(bf16[16,128,1024]{2,1,0:T(8,128)(2,1)} %bitcast.84, s32[1024]{0:T(1024)S(1)} %pad_clamp_fusion.1), kind=kCustom, calls=%fused_computation.2.clone | custom fusion | bytes 16777344 | tf_op jit(solution)/shard_map/jit(_take)/gather | solution.py:157
  324.0 7.5 %broadcast_select_fusion = bf16[32,128,1024]{2,1,0:T(8,128)(2,1)} fusion(bf16[32,128,1024]{2,1,0:T(8,128)(2,1)} %gather_fusion.2, pred[32]{0:T(512)(128)(4,1)S(1)} %compare_and_fusion.1), kind=kLoop, calls=%fused_computation.11 | loop fusion | flops 4194304 | bytes 16777248 | tf_op jit(solution)/shard_map/jit(_take)/select_n | solution.py:157
  331.6 9.8 %all-to-all-start.1 = ((bf16[32,128,1024]{2,1,0:T(8,128)(2,1)}), bf16[32,128,1024]{2,1,0:T(8,128)(2,1)}, u32[]{:S(2)}, u32[]{:S(2)}) async-start(bf16[32,128,1024]{2,1,0:T(8,128)(2,1)} %broadcast_select_fusion), calls=%async_computation.1 | async-start | bytes 16777216 | tf_op jit(solution)/shard_map/all_to_all | solution.py:158
  341.6 129.1 %all-to-all-done.1 = bf16[32,128,1024]{2,1,0:T(8,128)(2,1)} async-done(((bf16[32,128,1024]{2,1,0:T(8,128)(2,1)}), bf16[32,128,1024]{2,1,0:T(8,128)(2,1)}, u32[]{:S(2)}, u32[]{:S(2)}) %all-to-all-start.1) | async-done | bytes 8388640 | tf_op jit(solution)/shard_map/all_to_all | solution.py:158
  470.8 6.2 gather_fusion.3
  477.0 4.7 broadcast_select_fusion.2
  483.4 43.4 %reduce-scatter.11.cloned.1.call-done = bf16[64,512]{1,0:T(8,128)(2,1)} async-done(((bf16[1024,512]{1,0:T(8,128)(2,1)}), bf16[64,512]{1,0:T(8,128)(2,1)}) %reduce-scatter.11.cloned.1.call-update) | async-done | bytes 65552 | tf_op jit(solution)/shard_map/reduce_scatter | solution.py:170
  528.2 79.4 %reduce-scatter.7.cloned.1.call-done = bf16[512,256]{1,0:T(8,128)(2,1)} async-done(((bf16[512,4096]{1,0:T(8,128)(2,1)}), bf16[512,256]{1,0:T(8,128)(2,1)}) %reduce-scatter.7.cloned.1.call-update) | async-done | bytes 262160 | tf_op jit(solution)/shard_map/reduce_scatter | solution.py:164
  609.4 36.8 %reduce-scatter.5.cloned.1.call-done = bf16[2,128,1024]{2,1,0:T(8,128)(2,1)} async-done(((bf16[16,128,1024]{2,1,0:T(8,128)(2,1)}), bf16[2,128,1024]{2,1,0:T(8,128)(2,1)}) %reduce-scatter.5.cloned.1.call-update) | async-done | bytes 524304 | tf_op jit(solution)/shard_map/reduce_scatter | solution.py:160
  (107 shorter events, 62.3 us)
Async XLA Ops:
  7.2 14.4 %copy-start = (bf16[1024,1024]{1,0:T(8,128)(2,1)S(1)}, bf16[1024,1024]{1,0:T(8,128)(2,1)}, u32[]{:S(2)}) copy-start(bf16[1024,1024]{1,0:T(8,128)(2,1)} %param.27) | copy-start | bytes 6291460
  7.2 52.0 %all-gather.2.cloned.1.call-start = ((), (), s32[]{:S(2)}) async-start(), calls=%async_computation.6 | async-start | bytes 4718592 | tf_op jit(solution)/shard_map/all_gather | solution.py:123
  19.5 2.1 copy-start.2
  21.6 1.6 copy-start.12
  73.7 10.5 %copy-start.16 = (f32[4096]{0:T(1024)S(1)}, f32[4096]{0:T(1024)}, u32[]{:S(2)}) copy-start(f32[4096]{0:T(1024)} %param.20) | copy-start | bytes 49156
  73.7 153.9 %all-to-all-start = ((bf16[32,128,1024]{2,1,0:T(8,128)(2,1)}), bf16[32,128,1024]{2,1,0:T(8,128)(2,1)}, u32[]{:S(2)}, u32[]{:S(2)}) async-start(bf16[32,128,1024]{2,1,0:T(8,128)(2,1)} %broadcast_select_fusion.1), calls=%async_computation | async-start | bytes 16777216 | tf_op jit(solution)/shard_map/all_to_all | solution.py:125
  80.4 401.3 %reduce-scatter.9.cloned.1.call-start = ((), (), s32[]{:S(2)}) async-start(), calls=%async_computation.9 | async-start | bytes 1114112 | tf_op jit(solution)/shard_map/reduce_scatter | solution.py:167
  81.0 3.5 copy-start.3
  233.8 4.7 copy-start.14
  236.5 1.9 copy-start.5
  255.0 2.2 copy-start.11
  278.3 2.9 copy-start.6
  279.0 1.3 copy-start.8
  284.6 242.1 %reduce-scatter.11.cloned.1.call-start = ((), (), s32[]{:S(2)}) async-start(), calls=%async_computation.10 | async-start | bytes 1114112 | tf_op jit(solution)/shard_map/reduce_scatter | solution.py:170
  288.8 2.9 copy-start.7
  289.5 1.4 copy-start.10
  295.2 312.4 %reduce-scatter.7.cloned.1.call-start = ((), (), s32[]{:S(2)}) async-start(), calls=%async_computation.8 | async-start | bytes 4456448 | tf_op jit(solution)/shard_map/reduce_scatter | solution.py:164
  295.3 3.1 copy-start.9
  295.3 3.1 copy-start.13
  298.4 5.7 copy-start.4
  304.1 4.3 copy-start.15
  331.6 139.2 %all-to-all-start.1 = ((bf16[32,128,1024]{2,1,0:T(8,128)(2,1)}), bf16[32,128,1024]{2,1,0:T(8,128)(2,1)}, u32[]{:S(2)}, u32[]{:S(2)}) async-start(bf16[32,128,1024]{2,1,0:T(8,128)(2,1)} %broadcast_select_fusion), calls=%async_computation.1 | async-start | bytes 16777216 | tf_op jit(solution)/shard_map/all_to_all | solution.py:158
  341.4 304.8 %reduce-scatter.5.cloned.1.call-start = ((), (), s32[]{:S(2)}) async-start(), calls=%async_computation.7 | async-start | bytes 4718592 | tf_op jit(solution)/shard_map/reduce_scatter | solution.py:160
  481.7 166.7 %copy-start.1 = (bf16[1024,1024]{1,0:T(8,128)(2,1)S(1)}, bf16[1024,1024]{1,0:T(8,128)(2,1)}, u32[]{:S(2)}) copy-start(bf16[1024,1024]{1,0:T(8,128)(2,1)} %param.27) | copy-start | bytes 6291460
Sparse Core Ops, SparseCore 0:
  23.3 35.8 all-gather.1
  284.7 121.8 reduce-scatter.8
  409.9 116.8 reduce-scatter.10
  529.9 77.7 reduce-scatter.6
  609.9 36.2 reduce-scatter.4
where the time goes:
time: 664 us; the launch traced here: 655 us
  waiting for transfers between devices  456 us (69%)
  matrix products  82 us (12%)
  local copies, waits for them, and re-layouts  48.9 us (7%)
  other arithmetic  36.3 us (5%)
  starting transfers between devices  17.4 us (3%)
  between operations  14.4 us (2%)
    all_to_all x1, waiting for transfers between devices, local(): lax.all_to_all(outgoing, 'gen', split_axis=0, concat_axis=0, tiled=True)  132 us
    all_to_all x1, waiting for transfers between devices, local(): lax.all_to_all(returning, 'gen', split_axis=0, concat_axis=0, tiled=True)  129 us
    reduce_scatter x1, waiting for transfers between devices, local(): lax.psum_scatter(out_term.astype(jnp.bfloat16), 'gen', scatter_dimension=...  79.4 us
    reduce_scatter x1, waiting for transfers between devices, local(): lax.psum_scatter(value_term.astype(jnp.bfloat16), 'gen', scatter_dimensio...  43.4 us
    reduce_scatter x1, waiting for transfers between devices, local(): lax.psum_scatter(row_grads.astype(jnp.bfloat16), 'enc', scatter_dimension...  36.8 us
    all_gather x1, waiting for transfers between devices, local(): row_encoded = lax.all_gather(encoded, 'enc', axis=0, tiled=True)  34.8 us
    dot_general x1, matrix products, attention_grads(): jnp.einsum('bhqk,bqhd->bkhd', d_raw, queries, preferred_element_type=jnp....  16 us
  transfers between devices with their start and end apart: 7, of which 6 were waited for; matrix products, arithmetic and copies ran while one was open for 12% of the time, Pallas kernels for 0%

commit v1 on v0

--- a/solution.py
+++ b/solution.py
@@ -91,6 +91,19 @@
     return (send_column, column_position, receive_position, position_slot)
 
 
+def to_blocks(rows, enc_count, block_count, head_count):
+    features = rows.shape[1]
+    keys = rows.shape[0] // block_count
+    rows = rows.reshape(enc_count, block_count, keys // enc_count, features)
+    return rows.transpose(1, 0, 2, 3).reshape(block_count, keys, head_count, features // head_count)
+
+
+def from_blocks(blocks, enc_count):
+    block_count, keys, head_count, head_width = blocks.shape
+    rows = blocks.reshape(block_count, enc_count, keys // enc_count, head_count * head_width)
+    return rows.transpose(1, 0, 2, 3).reshape(block_count * keys, head_count * head_width)
+
+
 def local(
     hidden_states,
     grad_out,
@@ -119,11 +132,15 @@
     send_column, column_position, receive_position, position_slot = routing(
         nbr_index, row_index, gen_count, per_device, row_size, capacity
     )
+    chunk = length // enc_count
     encoded = encode(nbr_embed, enc_gain, enc_qkv, enc_out)
-    row_encoded = lax.all_gather(encoded, "enc", axis=0, tiled=True)
-    outgoing = jnp.take(row_encoded, send_column, axis=0)
+    pieces = encoded.reshape(per_device, enc_count, chunk, enc_width).transpose(1, 0, 2, 3)
+    columns = lax.all_to_all(pieces, "enc", split_axis=0, concat_axis=0, tiled=True)
+    columns = columns.reshape(row_size, chunk, enc_width)
+    outgoing = jnp.take(columns, send_column, axis=0)
     incoming = lax.all_to_all(outgoing, "gen", split_axis=0, concat_axis=0, tiled=True)
-    slot_encoded = jnp.take(incoming, receive_position, axis=0)
+    slot_pieces = jnp.take(incoming, receive_position, axis=0)
+    slot_encoded = lax.all_gather(slot_pieces, "enc", axis=0, tiled=False)
     slot_rows = slot_encoded.reshape(row_size * length, enc_width)
     normed = rms_scale(hidden_states, gain)
     queries = jnp.dot(normed, w_query, preferred_element_type=jnp.float32).astype(jnp.bfloat16)
@@ -132,8 +149,8 @@
     values_all = jnp.dot(slot_rows, w_value, preferred_element_type=jnp.float32).astype(
         jnp.bfloat16
     )
-    keys_all = keys_all.reshape(block_count, K * length, head_count, head_width)
-    values_all = values_all.reshape(block_count, K * length, head_count, head_width)
+    keys_all = to_blocks(keys_all, enc_count, block_count, head_count)
+    values_all = to_blocks(values_all, enc_count, block_count, head_count)
     raw_scores, probs_full, probs_low, mixed = attention_parts(queries, keys_all, values_all)
     mixed_rows = mixed.reshape(token_count, head_feats)
     d_mixed = jnp.dot(grad_out, w_out.T, preferred_element_type=jnp.float32).astype(jnp.bfloat16)
@@ -146,20 +163,28 @@
         probs_low,
         d_mixed.reshape(block_count, CH, head_count, head_width),
     )
-    d_keys_rows = d_keys.reshape(row_size * length, head_feats)
-    d_values_rows = d_values.reshape(row_size * length, head_feats)
+    d_keys_rows = from_blocks(d_keys, enc_count)
+    d_values_rows = from_blocks(d_values, enc_count)
     key_term = jnp.dot(slot_rows.T, d_keys_rows, preferred_element_type=jnp.float32)
     value_term = jnp.dot(slot_rows.T, d_values_rows, preferred_element_type=jnp.float32)
     enc_term = jnp.dot(d_keys_rows, w_key.T, preferred_element_type=jnp.float32) + jnp.dot(
         d_values_rows, w_value.T, preferred_element_type=jnp.float32
     )
-    enc_term_low = enc_term.astype(jnp.bfloat16).reshape(row_size, length, enc_width)
-    returning = jnp.take(enc_term_low, position_slot, axis=0)
+    enc_term_low = enc_term.astype(jnp.bfloat16).reshape(enc_count, row_size, chunk, enc_width)
+    summed = lax.psum_scatter(enc_term_low, "enc", scatter_dimension=0, tiled=False)
+    returning = jnp.take(summed, position_slot, axis=0)
     returned = lax.all_to_all(returning, "gen", split_axis=0, concat_axis=0, tiled=True)
-    row_grads = jnp.take(returned, column_position, axis=0).astype(jnp.float32)
-    grad_encoded = lax.psum_scatter(
-        row_grads.astype(jnp.bfloat16), "enc", scatter_dimension=0, tiled=True
-    ).astype(jnp.float32)
+    row_grads = jnp.take(returned, column_position, axis=0)
+    home = lax.all_to_all(
+        row_grads.reshape(enc_count, per_device, chunk, enc_width),
+        "enc",
+        split_axis=0,
+        concat_axis=0,
+        tiled=True,
+    )
+    grad_encoded = (
+        home.transpose(1, 0, 2, 3).reshape(per_device, length, enc_width).astype(jnp.float32)
+    )
     grad_w_out, grad_w_key, grad_w_value = (
         lax.psum_scatter(
             out_term.astype(jnp.bfloat16), "gen", scatter_dimension=1, tiled=True

time: 664 us -> 452 us (0.68)
  waiting for transfers between devices: 456 us -> 267 us
  other arithmetic: 36.3 us -> 16.8 us
  starting transfers between devices: 17.4 us -> 32 us
  local copies, waits for them, and re-layouts: 48.9 us -> 41.1 us
    all_to_all x1, waiting for transfers between devices: 132 us -> 15.3 us  [local(): lax.all_to_all(outgoing, 'gen', split_axis=0, concat_axis=0, tiled=True)]
    all_to_all x1, waiting for transfers between devices: 129 us -> 12.1 us  [local(): lax.all_to_all(returning, 'gen', split_axis=0, concat_axis=0, tiled=True)]
    reduce_scatter x1, waiting for transfers between devices: 0.02 us -> 46.9 us  [local(): lax.psum_scatter(key_term.astype(jnp.bfloat16), 'gen', scatter_dimension=...]
    reduce_scatter x1, waiting for transfers between devices: 43.4 us -> 74.7 us  [local(): lax.psum_scatter(value_term.astype(jnp.bfloat16), 'gen', scatter_dimensio...]
    gather x4, local copies, waits for them, and re-layouts: 26.6 us -> 3.42 us  [the longest x1 1.65 us: local(): returning = jnp.take(summed, position_slot, axis=0)]
    reduce_scatter x1, waiting for transfers between devices: 36.8 us -> 14.2 us  [local(): lax.psum_scatter(enc_term_low, 'enc', scatter_dimension=0, tiled=False)]
    all_gather x1, waiting for transfers between devices: 34.8 us -> 16.3 us  [local(): slot_encoded = lax.all_gather(slot_pieces, 'enc', axis=0, tiled=False)]
    select_n x8, other arithmetic: 22.4 us -> 4.11 us  [the longest x2 1.14 us: local(): returning = jnp.take(summed, position_slot, axis=0)]
  transfers between devices with their start and end apart: 7 -> 9, of which waited for: 6 -> 8; matrix products, arithmetic and copies ran while one was open for 12% -> 10% of each run, Pallas kernels for 0% -> 0%
where the time goes in v1:
time: 452 us; the launch traced here: 450 us
  waiting for transfers between devices  267 us (59%)
  matrix products  78.6 us (17%)
  local copies, waits for them, and re-layouts  41.1 us (9%)
  starting transfers between devices  32 us (7%)
  other arithmetic  16.8 us (4%)
  between operations  14.2 us (3%)
    reduce_scatter x1, waiting for transfers between devices, local(): lax.psum_scatter(out_term.astype(jnp.bfloat16), 'gen', scatter_dimension=...  79.3 us
    reduce_scatter x1, waiting for transfers between devices, local(): lax.psum_scatter(value_term.astype(jnp.bfloat16), 'gen', scatter_dimensio...  74.7 us
    reduce_scatter x1, waiting for transfers between devices, local(): lax.psum_scatter(key_term.astype(jnp.bfloat16), 'gen', scatter_dimension=...  46.9 us
    all_gather x1, waiting for transfers between devices, local(): slot_encoded = lax.all_gather(slot_pieces, 'enc', axis=0, tiled=False)  16.3 us
    dot_general x1, matrix products, attention_grads(): jnp.einsum('bhqk,bqhd->bkhd', d_raw, queries, preferred_element_type=jnp....  16.1 us
    all_to_all x1, waiting for transfers between devices, local(): lax.all_to_all(outgoing, 'gen', split_axis=0, concat_axis=0, tiled=True)  15.3 us
    reduce_scatter x1, waiting for transfers between devices, local(): lax.psum_scatter(enc_term_low, 'enc', scatter_dimension=0, tiled=False)  14.2 us
    all_to_all x1, waiting for transfers between devices, local(): lax.all_to_all(returning, 'gen', split_axis=0, concat_axis=0, tiled=True)  12.1 us
  transfers between devices with their start and end apart: 9, of which 8 were waited for; matrix products, arithmetic and copies ran while one was open for 10% of the time, Pallas kernels for 0%

profile of v1, /device:TPU:1, one launch (start us, length us, event | category | flops | bytes accessed | tf_op | source)
XLA Modules:
  0.0 449.6 jit_solution(1048881461592781112)
XLA Ops:
  9.8 4.6 %fusion.23 = bf16[32,8,24,128]{3,1,2,0:T(8,128)(2,1)S(1)} fusion(bf16[256,1024]{1,0:T(8,128)(2,1)S(1)} %bitcast.120, bf16[1024,3072]{1,0:T(8,128)(2,1)} %param.26), kind=kOutput, calls=%fused_computation.40 | convolution fusion | flops 1611399168 | bytes 8388608 | tf_op jit(solution)/shard_map/dot_general | solution.py:55
  23.2 6.8 %all-to-all-start = ((bf16[8,2,16,1024]{3,2,1,0:T(8,128)(2,1)}), bf16[8,2,16,1024]{3,2,1,0:T(8,128)(2,1)S(1)}, u32[]{:S(2)}, u32[]{:S(2)}) async-start(bf16[8,2,16,1024]{3,2,1,0:T(8,128)(2,1)} %bitcast.96), calls=%async_computation | async-start | bytes 1048576 | tf_op jit(solution)/shard_map/all_to_all | solution.py:138
  31.2 8.1 %all-to-all-done = bf16[8,2,16,1024]{3,2,1,0:T(8,128)(2,1)S(1)} async-done(((bf16[8,2,16,1024]{3,2,1,0:T(8,128)(2,1)}), bf16[8,2,16,1024]{3,2,1,0:T(8,128)(2,1)S(1)}, u32[]{:S(2)}, u32[]{:S(2)}) %all-to-all-start) | async-done | bytes 524320 | tf_op jit(solution)/shard_map/all_to_all | solution.py:138
  41.1 6.8 %all-to-all-start.1 = ((bf16[32,16,1024]{2,1,0:T(8,128)(2,1)}), bf16[32,16,1024]{2,1,0:T(8,128)(2,1)S(1)}, u32[]{:S(2)}, u32[]{:S(2)}) async-start(bf16[32,16,1024]{2,1,0:T(8,128)(2,1)} %broadcast_select_fusion.1), calls=%async_computation.1 | async-start | bytes 2097152 | tf_op jit(solution)/shard_map/all_to_all | solution.py:141
  48.0 15.3 %all-to-all-done.1 = bf16[32,16,1024]{2,1,0:T(8,128)(2,1)S(1)} async-done(((bf16[32,16,1024]{2,1,0:T(8,128)(2,1)}), bf16[32,16,1024]{2,1,0:T(8,128)(2,1)S(1)}, u32[]{:S(2)}, u32[]{:S(2)}) %all-to-all-start.1) | async-done | bytes 1048608 | tf_op jit(solution)/shard_map/all_to_all | solution.py:141
  68.5 4.6 %fusion.35 = bf16[512,512]{1,0:T(8,128)(2,1)S(1)} fusion(bf16[4096,512]{1,0:T(8,128)(2,1)} %param.21, bf16[512,4096]{1,0:T(8,128)(2,1)S(1)} %copy-done.3, f32[4096]{0:T(1024)S(1)} %copy-done.11, f32[512]{0:T(512)S(1)} %add_rsqrt_fusion), kind=kOutput, calls=%fused_computation.49 | convolution fusion | flops 2156134400 | bytes 8931328 | tf_op jit(solution)/shard_map/dot_general | solution.py:146
  73.2 6.1 %convolution_convert_fusion.6 = bf16[512,512]{1,0:T(8,128)(2,1)S(1)} fusion(bf16[512,4096]{1,0:T(8,128)(2,1)} %param.17, bf16[512,4096]{1,0:T(8,128)(2,1)} %param.22), kind=kOutput, calls=%fused_computation.50 | convolution fusion | flops 2147745792 | bytes 8912896 | tf_op jit(solution)/shard_map/dot_general | solution.py:156
  79.5 16.3 %all-gather.3.cloned.1.call-done = bf16[128,16,1024]{2,1,0:T(8,128)(2,1)} async-done(((bf16[16,16,1024]{2,1,0:T(8,128)(2,1)}), bf16[128,16,1024]{2,1,0:T(8,128)(2,1)}) %all-gather.3.cloned.1.call-update) | async-done | bytes 4194320 | tf_op jit(solution)/shard_map/all_gather | solution.py:143
  95.7 4.8 %convolution_convert_fusion.2 = bf16[2048,512]{1,0:T(8,128)(2,1)S(1)} fusion(bf16[2048,1024]{1,0:T(8,128)(2,1)} %bitcast.122, bf16[1024,512]{1,0:T(8,128)(2,1)} %param.24), kind=kOutput, calls=%fused_computation.16 | convolution fusion | flops 2148532224 | bytes 7340032 | tf_op jit(solution)/shard_map/dot_general | solution.py:149
  104.7 4.8 %convolution_convert_fusion.3 = bf16[2048,512]{1,0:T(8,128)(2,1)S(1)} fusion(bf16[2048,1024]{1,0:T(8,128)(2,1)} %bitcast.123, bf16[1024,512]{1,0:T(8,128)(2,1)} %param.23), kind=kOutput, calls=%fused_computation.17 | convolution fusion | flops 2148532224 | bytes 7340032 | tf_op jit(solution)/shard_map/dot_general | solution.py:148
  121.9 16.1 %convert_bitcast_fusion.1 = bf16[8,256,4,128]{1,3,2,0:T(8,128)(2,1)} fusion(f32[8,4,64,256]{3,2,1,0:T(8,128)} %fusion.19, f32[8,4,64,256]{3,2,1,0:T(8,128)} %copy-done.12, bf16[8,64,4,128]{3,2,1,0:T(4,128)(2,1)S(1)} %reshape.241, f32[8,4,64]{2,1,0:T(4,128)S(1)} %get-tuple-element.14), kind=kOutput, calls=%fused_computation.25 | convolution fusion | flops 142608640 | bytes 6823936 | tf_op jit(solution)/shard_map/bhqk,bqhd->bkhd/dot_general | solution.py:43
  138.0 4.2 copy.120
  149.5 4.2 copy.117
  162.3 4.5 add_convert_fusion
  166.9 6.2 %convolution_convert_fusion.5 = bf16[1024,512]{1,0:T(8,128)(2,1)} fusion(bf16[2048,1024]{1,0:T(8,128)(2,1)} %bitcast.124, bf16[2048,512]{1,0:T(8,128)(2,1)} %bitcast.113), kind=kOutput, calls=%fused_computation.42 | convolution fusion | flops 2148007936 | bytes 7340032 | tf_op jit(solution)/shard_map/dot_general | solution.py:168
  173.1 6.6 %convolution_convert_fusion.4 = bf16[1024,512]{1,0:T(8,128)(2,1)} fusion(bf16[2048,1024]{1,0:T(8,128)(2,1)} %bitcast.125, bf16[2048,512]{1,0:T(8,128)(2,1)} %bitcast.110), kind=kOutput, calls=%fused_computation.41 | convolution fusion | flops 2148007936 | bytes 7340032 | tf_op jit(solution)/shard_map/dot_general | solution.py:169
  183.0 4.3 convolution_convert_fusion
  187.4 14.2 %reduce-scatter.5.cloned.1.call-done = bf16[1,16,16,1024]{3,2,1,0:T(8,128)(2,1)} async-done(((bf16[8,16,16,1024]{3,2,1,0:T(8,128)(2,1)}), bf16[1,16,16,1024]{3,2,1,0:T(8,128)(2,1)}) %reduce-scatter.5.cloned.1.call-update) | async-done | bytes 524304 | tf_op jit(solution)/shard_map/reduce_scatter | solution.py:174
  204.4 6.5 %all-to-all-start.2 = ((bf16[32,16,1024]{2,1,0:T(8,128)(2,1)}), bf16[32,16,1024]{2,1,0:T(8,128)(2,1)S(1)}, u32[]{:S(2)}, u32[]{:S(2)}) async-start(bf16[32,16,1024]{2,1,0:T(8,128)(2,1)} %broadcast_select_fusion), calls=%async_computation.3 | async-start | bytes 2097152 | tf_op jit(solution)/shard_map/all_to_all | solution.py:176
  211.1 12.1 %all-to-all-done.2 = bf16[32,16,1024]{2,1,0:T(8,128)(2,1)S(1)} async-done(((bf16[32,16,1024]{2,1,0:T(8,128)(2,1)}), bf16[32,16,1024]{2,1,0:T(8,128)(2,1)S(1)}, u32[]{:S(2)}, u32[]{:S(2)}) %all-to-all-start.2) | async-done | bytes 1048608 | tf_op jit(solution)/shard_map/all_to_all | solution.py:176
  224.7 11.5 %all-to-all-start.3 = ((bf16[8,2,16,1024]{3,2,1,0:T(8,128)(2,1)}), bf16[8,2,16,1024]{3,2,1,0:T(8,128)(2,1)S(1)}, u32[]{:S(2)}, u32[]{:S(2)}) async-start(bf16[8,2,16,1024]{3,2,1,0:T(8,128)(2,1)} %bitcast.26), calls=%async_computation.4 | async-start | bytes 1048576 | tf_op jit(solution)/shard_map/all_to_all | solution.py:178
  236.3 46.9 %reduce-scatter.9.cloned.1.call-done = bf16[64,512]{1,0:T(8,128)(2,1)} async-done(((bf16[1024,512]{1,0:T(8,128)(2,1)}), bf16[64,512]{1,0:T(8,128)(2,1)}) %reduce-scatter.9.cloned.1.call-update) | async-done | bytes 65552 | tf_op jit(solution)/shard_map/reduce_scatter | solution.py:192
  284.7 74.7 %reduce-scatter.11.cloned.1.call-done = bf16[64,512]{1,0:T(8,128)(2,1)} async-done(((bf16[1024,512]{1,0:T(8,128)(2,1)}), bf16[64,512]{1,0:T(8,128)(2,1)}) %reduce-scatter.11.cloned.1.call-update) | async-done | bytes 65552 | tf_op jit(solution)/shard_map/reduce_scatter | solution.py:195
  360.9 79.3 %reduce-scatter.7.cloned.1.call-done = bf16[512,256]{1,0:T(8,128)(2,1)} async-done(((bf16[512,4096]{1,0:T(8,128)(2,1)}), bf16[512,256]{1,0:T(8,128)(2,1)}) %reduce-scatter.7.cloned.1.call-update) | async-done | bytes 262160 | tf_op jit(solution)/shard_map/reduce_scatter | solution.py:189
  (108 shorter events, 65.8 us)
Async XLA Ops:
  7.2 14.4 %copy-start = (bf16[1024,1024]{1,0:T(8,128)(2,1)S(1)}, bf16[1024,1024]{1,0:T(8,128)(2,1)}, u32[]{:S(2)}) copy-start(bf16[1024,1024]{1,0:T(8,128)(2,1)} %param.27) | copy-start | bytes 6291460
  19.5 2.1 copy-start.2
  21.6 8.4 %copy-start.8 = (s32[128,2]{0,1:T(2,128)S(1)}, s32[128,2]{0,1:T(2,128)}, u32[]{:S(2)}) copy-start(s32[128,2]{0,1:T(2,128)} %param.19) | copy-start | bytes 3076
  23.2 16.1 %all-to-all-start = ((bf16[8,2,16,1024]{3,2,1,0:T(8,128)(2,1)}), bf16[8,2,16,1024]{3,2,1,0:T(8,128)(2,1)S(1)}, u32[]{:S(2)}, u32[]{:S(2)}) async-start(bf16[8,2,16,1024]{3,2,1,0:T(8,128)(2,1)} %bitcast.96), calls=%async_computation | async-start | bytes 1048576 | tf_op jit(solution)/shard_map/all_to_all | solution.py:138
  41.1 22.2 %all-to-all-start.1 = ((bf16[32,16,1024]{2,1,0:T(8,128)(2,1)}), bf16[32,16,1024]{2,1,0:T(8,128)(2,1)S(1)}, u32[]{:S(2)}, u32[]{:S(2)}) async-start(bf16[32,16,1024]{2,1,0:T(8,128)(2,1)} %broadcast_select_fusion.1), calls=%async_computation.1 | async-start | bytes 2097152 | tf_op jit(solution)/shard_map/all_to_all | solution.py:141
  47.8 47.9 %all-gather.3.cloned.1.call-start = ((), (), s32[]{:S(2)}) async-start(), calls=%async_computation.12 | async-start | bytes 4718592 | tf_op jit(solution)/shard_map/all_gather | solution.py:143
  64.8 3.5 copy-start.11
  64.8 136.8 %reduce-scatter.5.cloned.1.call-start = ((), (), s32[]{:S(2)}) async-start(), calls=%async_computation.8 | async-start | bytes 4718592 | tf_op jit(solution)/shard_map/reduce_scatter | solution.py:174
  65.1 3.5 copy-start.3
  115.0 2.2 copy-start.7
  118.2 1.4 copy-start.12
  157.9 1.9 copy-start.9
  159.7 2.4 copy-start.6
  159.7 2.4 copy-start.5
  159.7 2.6 copy-start.10
  166.8 116.4 %reduce-scatter.9.cloned.1.call-start = ((), (), s32[]{:S(2)}) async-start(), calls=%async_computation.10 | async-start | bytes 1114112 | tf_op jit(solution)/shard_map/reduce_scatter | solution.py:192
  173.1 186.3 %reduce-scatter.11.cloned.1.call-start = ((), (), s32[]{:S(2)}) async-start(), calls=%async_computation.11 | async-start | bytes 1114112 | tf_op jit(solution)/shard_map/reduce_scatter | solution.py:195
  179.8 260.4 %reduce-scatter.7.cloned.1.call-start = ((), (), s32[]{:S(2)}) async-start(), calls=%async_computation.9 | async-start | bytes 4456448 | tf_op jit(solution)/shard_map/reduce_scatter | solution.py:189
  179.9 3.1 copy-start.4
  204.4 18.8 %all-to-all-start.2 = ((bf16[32,16,1024]{2,1,0:T(8,128)(2,1)}), bf16[32,16,1024]{2,1,0:T(8,128)(2,1)S(1)}, u32[]{:S(2)}, u32[]{:S(2)}) async-start(bf16[32,16,1024]{2,1,0:T(8,128)(2,1)} %broadcast_select_fusion), calls=%async_computation.3 | async-start | bytes 2097152 | tf_op jit(solution)/shard_map/all_to_all | solution.py:176
  223.8 219.3 %copy-start.1 = (bf16[1024,1024]{1,0:T(8,128)(2,1)S(1)}, bf16[1024,1024]{1,0:T(8,128)(2,1)}, u32[]{:S(2)}) copy-start(bf16[1024,1024]{1,0:T(8,128)(2,1)} %param.27) | copy-start | bytes 6291460
  224.7 217.3 %all-to-all-start.3 = ((bf16[8,2,16,1024]{3,2,1,0:T(8,128)(2,1)}), bf16[8,2,16,1024]{3,2,1,0:T(8,128)(2,1)S(1)}, u32[]{:S(2)}, u32[]{:S(2)}) async-start(bf16[8,2,16,1024]{3,2,1,0:T(8,128)(2,1)} %bitcast.26), calls=%async_computation.4 | async-start | bytes 1048576 | tf_op jit(solution)/shard_map/all_to_all | solution.py:178
Sparse Core Ops, SparseCore 0:
  64.9 30.7 all-gather.2
  166.9 34.6 reduce-scatter.4
  204.8 78.3 reduce-scatter.8
  286.2 73.1 reduce-scatter.10
  362.6 77.6 reduce-scatter.6

commit v2 on v1

--- a/solution.py
+++ b/solution.py
@@ -1,12 +1,16 @@
 import jax
 import jax.numpy as jnp
 from jax import lax
+from jax.experimental import pallas as pl
+from jax.experimental.pallas import tpu as pltpu
 from jax.sharding import PartitionSpec as P
 
 H = 32
 EH = 8
 CH = 64
 K = 2
+
+MESH = pl.DeviceIdType.MESH
 
 
 SOFTCAP = 5.0
@@ -104,6 +108,393 @@
     return rows.transpose(1, 0, 2, 3).reshape(block_count * keys, head_count * head_width)
 
 
+def neighbours():
+    enc, gen = lax.axis_index("enc"), lax.axis_index("gen")
+    z, core, x, y = enc // 2, enc % 2, gen // 4, gen % 4
+
+    def at(axis, step):
+        if axis == "x":
+            return (enc, (x + step) % 4 * 4 + y)
+        if axis == "y":
+            return (enc, x * 4 + (y + step) % 4)
+        if axis == "z":
+            return ((z + step) % 4 * 2 + core, gen)
+        return (z * 2 + (1 - core), gen)
+
+    return enc, gen, {"x": x, "y": y, "z": z, "core": core}, at
+
+
+def entry_barrier(enc, gen):
+    barrier = pltpu.get_barrier_semaphore()
+
+    def greet_gen(step, carry):
+        pl.semaphore_signal(barrier, inc=1, device_id=(enc, (gen + step) % 16), device_id_type=MESH)
+        return carry
+
+    def greet_enc(step, carry):
+        pl.semaphore_signal(barrier, inc=1, device_id=((enc + step) % 8, gen), device_id_type=MESH)
+        return carry
+
+    lax.fori_loop(1, 16, greet_gen, 0)
+    lax.fori_loop(1, 8, greet_enc, 0)
+    pl.semaphore_wait(barrier, 22)
+
+
+def send(src, dst, sems, number, device):
+    return pltpu.make_async_remote_copy(
+        src_ref=src,
+        dst_ref=dst,
+        send_sem=sems.at[0, number],
+        recv_sem=sems.at[1, number],
+        device_id=device,
+        device_id_type=MESH,
+    )
+
+
+def add_rows(out, out_at, terms, rows, step):
+    def body(i, carry):
+        total = None
+        for ref, at in terms:
+            value = ref[pl.ds(pl.multiple_of(at + i * step, step), step), :].astype(jnp.float32)
+            total = value if total is None else total + value
+        if len(out.shape) == 3:
+            out[out_at + i] = total.astype(out.dtype)
+        else:
+            out[pl.ds(pl.multiple_of(out_at + i * step, step), step), :] = total.astype(out.dtype)
+        return carry
+
+    lax.fori_loop(0, rows // step, body, 0)
+
+
+class Ring:
+    def __init__(self, src, buf, sems, axis, where, at):
+        self.src, self.buf = src, buf
+        self.rows = src.shape[0] // 4
+        self.half = self.rows // 2
+        self.me = where[axis]
+        half = self.half
+        self.plus, self.minus = (self.me + 1) % 4, (self.me + 3) % 4
+        across = (self.me + 2) % 4
+        pieces = (
+            (across, 0, 1),
+            (self.plus, 1, 1),
+            (self.plus, 0, 1),
+            (across, 1, 3),
+            (self.minus, 0, 3),
+            (self.minus, 1, 3),
+        )
+        self.copies = []
+        for number, (chunk, side, step) in enumerate(pieces):
+            start = pl.multiple_of(chunk * self.rows + side * half, half)
+            self.copies.append(
+                send(
+                    src.at[pl.ds(start, half), :],
+                    buf.at[pl.ds(number * half, half), :],
+                    sems,
+                    number,
+                    at(axis, step),
+                )
+            )
+
+    def first(self):
+        self.copies[0].start()
+        self.copies[3].start()
+
+    def second(self):
+        self.copies[1].start()
+        self.copies[4].start()
+
+    def third(self, step):
+        half = self.half
+        self.copies[0].wait_recv()
+        start = self.plus * self.rows
+        add_rows(self.src, start, ((self.src, start), (self.buf, 0)), half, step)
+        self.copies[2].start()
+        self.copies[3].wait_recv()
+        start = self.minus * self.rows + half
+        add_rows(self.src, start, ((self.src, start), (self.buf, 3 * half)), half, step)
+        self.copies[5].start()
+
+    def last(self, out, out_at, step):
+        half = self.half
+        for number in (1, 2, 4, 5):
+            self.copies[number].wait_recv()
+        start = self.me * self.rows
+        add_rows(out, out_at, ((self.src, start), (self.buf, 2 * half), (self.buf, 4 * half)), half, step)
+        add_rows(
+            out, out_at + (half // step if len(out.shape) == 3 else half), ((self.src, start + half), (self.buf, half), (self.buf, 5 * half)), half, step
+        )
+
+    def drain(self):
+        for copy in self.copies:
+            copy.wait_send()
+
+
+def back_kernel(
+    position_ref, column_ref,
+    mixed_hbm, cot_hbm, rows_hbm, dk_hbm, dv_hbm, wk_hbm, wv_hbm,
+    enc_out, wo_out, wk_out, wv_out,
+    mixed, cot, rows, dk, dv, wk, wv, mixed_t,
+    ot_a, ot_b, kt, vt, ot_a2, ot_b2, kt2, vt2, peers, mine, from_peer, piece, outgoing, returned, grads, home,
+    b_ota, b_otb, b_kt, b_vt, b_ota2, b_otb2, b_kt2, b_vt2, b_z,
+    load_sems, s_ota, s_otb, s_kt, s_vt, s_ota2, s_otb2, s_kt2, s_vt2, s_z, s_core, s_gen, s_enc,
+):
+    loads = []
+    for number, (src, dst) in enumerate(
+        (
+            (mixed_hbm, mixed), (cot_hbm, cot), (dk_hbm, dk), (dv_hbm, dv),
+            (wk_hbm, wk), (wv_hbm, wv), (rows_hbm, rows),
+        )
+    ):
+        copy = pltpu.make_async_copy(src, dst, load_sems.at[number])
+        copy.start()
+        loads.append(copy)
+    enc, gen, where, at = neighbours()
+    x, y, z, core = where["x"], where["y"], where["z"], where["core"]
+    entry_barrier(enc, gen)
+    ring_oa = Ring(ot_a, b_ota, s_ota, "x", where, at)
+    ring_ob = Ring(ot_b, b_otb, s_otb, "y", where, at)
+    ring_k = Ring(kt, b_kt, s_kt, "x", where, at)
+    ring_v = Ring(vt, b_vt, s_vt, "y", where, at)
+    ring_oa2 = Ring(ot_a2, b_ota2, s_ota2, "y", where, at)
+    ring_ob2 = Ring(ot_b2, b_otb2, s_otb2, "x", where, at)
+    ring_k2 = Ring(kt2, b_kt2, s_kt2, "y", where, at)
+    ring_v2 = Ring(vt2, b_vt2, s_vt2, "x", where, at)
+    ring_z = Ring(mine, b_z, s_z, "z", where, at)
+
+    loads[0].wait()
+    mixed_t[...] = mixed[...].T
+    loads[1].wait()
+
+    def out_terms(i, carry):
+        to_x, to_y = (x + 2 - i + 4) % 4, (y + 2 - i + 4) % 4
+
+        def tile(j, carry):
+            lane_a = pl.multiple_of((to_x * 4 + j) * 256, 256)
+            term = jnp.dot(mixed_t[0:256, :], cot[:, pl.ds(lane_a, 256)], preferred_element_type=jnp.float32)
+            ot_a[pl.ds(pl.multiple_of(lane_a, 256), 256), :] = term.astype(jnp.bfloat16)
+            lane_b = pl.multiple_of((j * 4 + to_y) * 256, 256)
+            term = jnp.dot(mixed_t[256:512, :], cot[:, pl.ds(lane_b, 256)], preferred_element_type=jnp.float32)
+            ot_b[pl.ds(pl.multiple_of((to_y * 4 + j) * 256, 256), 256), :] = term.astype(jnp.bfloat16)
+            return carry
+
+        lax.fori_loop(0, 4, tile, 0)
+
+        @pl.when(i == 0)
+        def _():
+            ring_oa.first()
+            ring_ob.first()
+
+        return carry
+
+    lax.fori_loop(0, 4, out_terms, 0)
+    ring_oa.second()
+    ring_ob.second()
+
+    for number in (2, 3, 4, 5):
+        loads[number].wait()
+    core_copies = [
+        send(peers.at[pl.ds(k * 256, 256), :], from_peer.at[pl.ds(k * 256, 256), :], s_core, k, at("core", 1))
+        for k in range(4)
+    ]
+
+    def enc_piece(piece_at, out, out_at):
+        def tile(j, carry):
+            start = pl.multiple_of(piece_at * 256 + j * 128, 128)
+            term = lax.dot_general(
+                dk[pl.ds(start, 128), :], wk[...], (((1,), (1,)), ((), ())), preferred_element_type=jnp.float32
+            )
+            term = term + lax.dot_general(
+                dv[pl.ds(start, 128), :], wv[...], (((1,), (1,)), ((), ())), preferred_element_type=jnp.float32
+            )
+            out[pl.ds(pl.multiple_of(out_at + j * 128, 128), 128), :] = term.astype(jnp.bfloat16)
+            return carry
+
+        lax.fori_loop(0, 2, tile, 0)
+
+    def to_peer(k, carry):
+        enc_piece(k * 2 + (1 - core), peers, k * 256)
+        for number in range(4):
+
+            @pl.when(k == number)
+            def _():
+                core_copies[number].start()
+
+        return carry
+
+    lax.fori_loop(0, 4, to_peer, 0)
+
+    def to_own(k, carry):
+        enc_piece(k * 2 + core, mine, k * 256)
+        return carry
+
+    lax.fori_loop(0, 4, to_own, 0)
+    for k in range(4):
+        core_copies[k].wait_recv()
+    add_rows(mine, 0, ((mine, 0), (from_peer, 0)), 1024, 32)
+    ring_z.first()
+    ring_z.second()
+    ring_oa.third(64)
+    ring_ob.third(64)
+
+    loads[6].wait()
+
+    def key_terms(i, carry):
+        lane = pl.multiple_of(i * 128, 128)
+        block = rows[:, pl.ds(lane, 128)]
+        term = lax.dot_general(block, dk[...], (((0,), (0,)), ((), ())), preferred_element_type=jnp.float32)
+        kt[pl.ds(pl.multiple_of(i * 128, 128), 128), :] = term.astype(jnp.bfloat16)
+        term = lax.dot_general(block, dv[...], (((0,), (0,)), ((), ())), preferred_element_type=jnp.float32)
+        low = term.astype(jnp.bfloat16)
+        for part in range(2):
+            to_x, to_y = (i * 2 + part) // 4, (i * 2 + part) % 4
+            vt[pl.ds(pl.multiple_of(to_y * 256 + to_x * 64, 64), 64), :] = low[part * 64 : part * 64 + 64]
+        return carry
+
+    lax.fori_loop(0, 8, key_terms, 0)
+    ring_k.first()
+    ring_v.first()
+    ring_k.second()
+    ring_v.second()
+
+    ring_z.third(32)
+    ring_k.third(64)
+    ring_v.third(64)
+
+    ring_oa.last(ot_a2, 0, 64)
+    ring_oa2.first()
+    ring_oa2.second()
+    ring_ob.last(ot_b2, 0, 64)
+    ring_ob2.first()
+    ring_ob2.second()
+
+    ring_z.last(piece, 0, 16)
+    for j in range(32):
+        outgoing[j] = piece[position_ref[j]]
+    own_at = gen * 2
+
+    def gen_copy(step):
+        peer = (gen + step) % 16
+        return send(
+            outgoing.at[pl.ds(peer * 2, 2)],
+            returned.at[pl.ds(own_at, 2)],
+            s_gen,
+            step - 1,
+            (enc, peer),
+        )
+
+    def start_gen(step, carry):
+        gen_copy(step).start()
+        return carry
+
+    lax.fori_loop(1, 16, start_gen, 0)
+    returned[pl.ds(own_at, 2)] = outgoing[pl.ds(own_at, 2)]
+
+    ring_k.last(kt2, 0, 64)
+    ring_k2.first()
+    ring_k2.second()
+    ring_v.last(vt2, 0, 64)
+    ring_v2.first()
+    ring_v2.second()
+    ring_oa2.third(64)
+    ring_ob2.third(64)
+    ring_k2.third(32)
+    ring_v2.third(32)
+
+    def wait_gen(step, carry):
+        gen_copy(step).wait_recv()
+        return carry
+
+    lax.fori_loop(1, 16, wait_gen, 0)
+    for j in range(16):
+        grads[j // 2, j % 2] = returned[column_ref[j]]
+    row_at = pl.multiple_of(enc * 16, 16)
+
+    def enc_copy(step):
+        peer = (enc + step) % 8
+        return send(grads.at[peer], home.at[:, pl.ds(row_at, 16), :], s_enc, step - 1, (peer, gen))
+
+    def start_enc(step, carry):
+        enc_copy(step).start()
+        return carry
+
+    lax.fori_loop(1, 8, start_enc, 0)
+    home[:, pl.ds(row_at, 16), :] = grads[enc]
+
+    ring_oa2.last(wo_out, 0, 64)
+    ring_ob2.last(wo_out, 256, 64)
+    ring_k2.last(wk_out, 0, 32)
+    ring_v2.last(wv_out, 0, 32)
+
+    def wait_enc(step, carry):
+        enc_copy(step).wait_recv()
+        return carry
+
+    lax.fori_loop(1, 8, wait_enc, 0)
+    enc_out[...] = home[...]
+
+    for ring in (ring_oa, ring_ob, ring_k, ring_v, ring_oa2, ring_ob2, ring_k2, ring_v2, ring_z):
+        ring.drain()
+    for k in range(4):
+        core_copies[k].wait_send()
+
+    def drain_gen(step, carry):
+        gen_copy(step).wait_send()
+        return carry
+
+    def drain_enc(step, carry):
+        enc_copy(step).wait_send()
+        return carry
+
+    lax.fori_loop(1, 16, drain_gen, 0)
+    lax.fori_loop(1, 8, drain_enc, 0)
+
+
+def back(position, column, mixed, cot, rows, dk, dv, wk, wv):
+    low = jnp.bfloat16
+
+    def ring_buffer(src):
+        return pltpu.VMEM((src[0] // 4 * 3, src[1]), low)
+
+    srcs = ((4096, 256), (4096, 256), (1024, 512), (1024, 512), (1024, 256), (1024, 256), (256, 512), (256, 512))
+    anywhere = pl.BlockSpec(memory_space=pl.ANY)
+    scalars = pl.BlockSpec(memory_space=pltpu.SMEM)
+    whole = pl.BlockSpec(memory_space=pltpu.VMEM)
+    operands = (mixed, cot, rows, dk, dv, wk, wv)
+    return pl.pallas_call(
+        back_kernel,
+        out_shape=(
+            jax.ShapeDtypeStruct((2, 128, 1024), low),
+            jax.ShapeDtypeStruct((512, 256), low),
+            jax.ShapeDtypeStruct((64, 512), low),
+            jax.ShapeDtypeStruct((64, 512), low),
+        ),
+        in_specs=[scalars] * 2 + [anywhere] * 7,
+        out_specs=(whole,) * 4,
+        scratch_shapes=[pltpu.VMEM(a.shape, low) for a in operands]
+        + [pltpu.VMEM((512, 512), low)]
+        + [pltpu.VMEM(s, low) for s in srcs]
+        + [
+            pltpu.VMEM((1024, 1024), low),
+            pltpu.VMEM((1024, 1024), low),
+            pltpu.VMEM((1024, 1024), low),
+            pltpu.VMEM((16, 16, 1024), low),
+            pltpu.VMEM((32, 16, 1024), low),
+            pltpu.VMEM((32, 16, 1024), low),
+            pltpu.VMEM((8, 2, 16, 1024), low),
+            pltpu.VMEM((2, 128, 1024), low),
+        ]
+        + [ring_buffer(s) for s in srcs]
+        + [ring_buffer((1024, 1024))]
+        + [pltpu.SemaphoreType.DMA((7,))]
+        + [pltpu.SemaphoreType.DMA((2, 6))] * 9
+        + [pltpu.SemaphoreType.DMA((2, 4)), pltpu.SemaphoreType.DMA((2, 15)), pltpu.SemaphoreType.DMA((2, 7))],
+        compiler_params=pltpu.CompilerParams(
+            collective_id=1, has_side_effects=True, vmem_limit_bytes=62 * 1024 * 1024
+        ),
+    )(position, column, *operands)
+
+
 def local(
     hidden_states,
     grad_out,
@@ -154,7 +545,6 @@
     raw_scores, probs_full, probs_low, mixed = attention_parts(queries, keys_all, values_all)
     mixed_rows = mixed.reshape(token_count, head_feats)
     d_mixed = jnp.dot(grad_out, w_out.T, preferred_element_type=jnp.float32).astype(jnp.bfloat16)
-    out_term = jnp.dot(mixed_rows.T, grad_out, preferred_element_type=jnp.float32)
     d_keys, d_values = attention_grads(
         queries,
         values_all,
@@ -165,38 +555,18 @@
     )
     d_keys_rows = from_blocks(d_keys, enc_count)
     d_values_rows = from_blocks(d_values, enc_count)
-    key_term = jnp.dot(slot_rows.T, d_keys_rows, preferred_element_type=jnp.float32)
-    value_term = jnp.dot(slot_rows.T, d_values_rows, preferred_element_type=jnp.float32)
-    enc_term = jnp.dot(d_keys_rows, w_key.T, preferred_element_type=jnp.float32) + jnp.dot(
-        d_values_rows, w_value.T, preferred_element_type=jnp.float32
-    )
-    enc_term_low = enc_term.astype(jnp.bfloat16).reshape(enc_count, row_size, chunk, enc_width)
-    summed = lax.psum_scatter(enc_term_low, "enc", scatter_dimension=0, tiled=False)
-    returning = jnp.take(summed, position_slot, axis=0)
-    returned = lax.all_to_all(returning, "gen", split_axis=0, concat_axis=0, tiled=True)
-    row_grads = jnp.take(returned, column_position, axis=0)
-    home = lax.all_to_all(
-        row_grads.reshape(enc_count, per_device, chunk, enc_width),
-        "enc",
-        split_axis=0,
-        concat_axis=0,
-        tiled=True,
-    )
-    grad_encoded = (
-        home.transpose(1, 0, 2, 3).reshape(per_device, length, enc_width).astype(jnp.float32)
-    )
-    grad_w_out, grad_w_key, grad_w_value = (
-        lax.psum_scatter(
-            out_term.astype(jnp.bfloat16), "gen", scatter_dimension=1, tiled=True
-        ).astype(jnp.float32),
-        lax.psum_scatter(
-            key_term.astype(jnp.bfloat16), "gen", scatter_dimension=0, tiled=True
-        ).astype(jnp.float32),
-        lax.psum_scatter(
-            value_term.astype(jnp.bfloat16), "gen", scatter_dimension=0, tiled=True
-        ).astype(jnp.float32),
-    )
-    return (grad_encoded, grad_w_out, grad_w_key, grad_w_value)
+    outputs = back(
+        position_slot,
+        column_position,
+        mixed_rows,
+        grad_out,
+        slot_rows,
+        d_keys_rows,
+        d_values_rows,
+        w_key,
+        w_value,
+    )
+    return tuple(output.astype(jnp.float32) for output in outputs)
 
 
 def solution(mesh):

time: 452 us -> 238 us (0.53)
  waiting for transfers between devices: 267 us -> 38.4 us
  Pallas kernels: 0 us -> 68.9 us
  matrix products: 78.6 us -> 53.6 us
  starting transfers between devices: 32 us -> 13.8 us
  local copies, waits for them, and re-layouts: 41.1 us -> 32.7 us
    reduce_scatter x4 -> x0, waiting for transfers between devices: 215 us -> none  [the longest x1 79.3 us: local(): lax.psum_scatter(out_term.astype(jnp.bfloat16), 'gen', scatter_dimension=...]
    pallas_call x0 -> x1, Pallas kernels: none -> 68.9 us  [back(): pl.pallas_call(back_kernel, out_shape=(jax.ShapeDtypeStruct((2, 128, 1024...]
    dot_general x5 -> x0, matrix products: 24 us -> none  [the longest x1 6.64 us: local(): jnp.dot(slot_rows.T, d_values_rows, preferred_element_type=jnp.float32)]
    all_to_all x2 -> x0, starting transfers between devices: 18.1 us -> none  [the longest x1 11.5 us: local(): lax.all_to_all(row_grads.reshape(enc_count, per_device, chunk, enc_width)...]
    all_to_all x2 -> x0, waiting for transfers between devices: 12.1 us -> none  [the longest x1 12.1 us: local(): lax.all_to_all(returning, 'gen', split_axis=0, concat_axis=0, tiled=True)]
  transfers between devices with their start and end apart: 9 -> 3, of which waited for: 8 -> 3; matrix products, arithmetic and copies ran while one was open for 10% -> 7% of each run, Pallas kernels for 0% -> 0%
where the time goes in v2:
time: 238 us; the launch traced here: 237 us
  Pallas kernels  68.9 us (29%)
  matrix products  53.6 us (23%)
  waiting for transfers between devices  38.4 us (16%)
  local copies, waits for them, and re-layouts  32.7 us (14%)
  other arithmetic  15 us (6%)
  between operations  14.3 us (6%)
  starting transfers between devices  13.8 us (6%)
    pallas_call x1, Pallas kernels, back(): pl.pallas_call(back_kernel, out_shape=(jax.ShapeDtypeStruct((2, 128, 1024...  68.9 us
    dot_general x1, matrix products, attention_grads(): jnp.einsum('bhqk,bqhd->bkhd', d_raw, queries, preferred_element_type=jnp....  16.3 us
    all_to_all x1, waiting for transfers between devices, local(): lax.all_to_all(outgoing, 'gen', split_axis=0, concat_axis=0, tiled=True)  15.1 us
    all_gather x1, waiting for transfers between devices, local(): slot_encoded = lax.all_gather(slot_pieces, 'enc', axis=0, tiled=False)  15.1 us
    all_to_all x1, waiting for transfers between devices, local(): lax.all_to_all(pieces, 'enc', split_axis=0, concat_axis=0, tiled=True)  8.1 us
    all_to_all x1, starting transfers between devices, local(): lax.all_to_all(pieces, 'enc', split_axis=0, concat_axis=0, tiled=True)  6.8 us
    all_to_all x1, starting transfers between devices, local(): lax.all_to_all(outgoing, 'gen', split_axis=0, concat_axis=0, tiled=True)  6.76 us
    reshape x2, local copies, waits for them, and re-layouts, to_blocks(): rows.transpose(1, 0, 2, 3)  6.53 us
  transfers between devices with their start and end apart: 3, of which 3 were waited for; matrix products, arithmetic and copies ran while one was open for 7% of the time, Pallas kernels for 0%

profile of v2, /device:TPU:1, one launch (start us, length us, event | category | flops | bytes accessed | tf_op | source)
XLA Modules:
  0.0 236.6 jit_solution(8845852965462733283)
XLA Ops:
  9.6 4.6 %fusion.23 = bf16[32,8,24,128]{3,1,2,0:T(8,128)(2,1)S(1)} fusion(bf16[256,1024]{1,0:T(8,128)(2,1)S(1)} %bitcast.110, bf16[1024,3072]{1,0:T(8,128)(2,1)} %param.22), kind=kOutput, calls=%fused_computation.36 | convolution fusion | flops 1611399168 | bytes 8388608 | tf_op jit(solution)/shard_map/dot_general | solution.py:59
  17.5 2.2 convolution_convert_fusion.4
  21.6 6.8 %all-to-all-start = ((bf16[8,2,16,1024]{3,2,1,0:T(8,128)(2,1)}), bf16[8,2,16,1024]{3,2,1,0:T(8,128)(2,1)S(1)}, u32[]{:S(2)}, u32[]{:S(2)}) async-start(bf16[8,2,16,1024]{3,2,1,0:T(8,128)(2,1)} %bitcast.87), calls=%async_computation | async-start | bytes 1048576 | tf_op jit(solution)/shard_map/all_to_all | solution.py:529
  29.7 8.1 %all-to-all-done = bf16[8,2,16,1024]{3,2,1,0:T(8,128)(2,1)S(1)} async-done(((bf16[8,2,16,1024]{3,2,1,0:T(8,128)(2,1)}), bf16[8,2,16,1024]{3,2,1,0:T(8,128)(2,1)S(1)}, u32[]{:S(2)}, u32[]{:S(2)}) %all-to-all-start) | async-done | bytes 524320 | tf_op jit(solution)/shard_map/all_to_all | solution.py:529
  39.5 6.8 %all-to-all-start.1 = ((bf16[32,16,1024]{2,1,0:T(8,128)(2,1)}), bf16[32,16,1024]{2,1,0:T(8,128)(2,1)S(1)}, u32[]{:S(2)}, u32[]{:S(2)}) async-start(bf16[32,16,1024]{2,1,0:T(8,128)(2,1)} %broadcast_select_fusion), calls=%async_computation.1 | async-start | bytes 2097152 | tf_op jit(solution)/shard_map/all_to_all | solution.py:532
  46.6 15.1 %all-to-all-done.1 = bf16[32,16,1024]{2,1,0:T(8,128)(2,1)S(1)} async-done(((bf16[32,16,1024]{2,1,0:T(8,128)(2,1)}), bf16[32,16,1024]{2,1,0:T(8,128)(2,1)S(1)}, u32[]{:S(2)}, u32[]{:S(2)}) %all-to-all-start.1) | async-done | bytes 1048608 | tf_op jit(solution)/shard_map/all_to_all | solution.py:532
  63.3 3.2 %fusion.1 = f32[512]{0:T(512)S(1)} fusion(bf16[512,4096]{1,0:T(8,128)(2,1)} %param.12), kind=kLoop, calls=%fused_computation.5 | loop fusion | flops 6290944 | bytes 4196352 | tf_op jit(solution)/shard_map/reduce_sum | solution.py:22
  66.7 4.6 %fusion.35 = bf16[512,512]{1,0:T(8,128)(2,1)S(1)} fusion(bf16[4096,512]{1,0:T(8,128)(2,1)} %param.17, bf16[512,4096]{1,0:T(8,128)(2,1)S(1)} %copy-done.1, f32[4096]{0:T(1024)S(1)} %copy-done.7, f32[512]{0:T(512)S(1)} %add_rsqrt_fusion), kind=kOutput, calls=%fused_computation.43 | convolution fusion | flops 2156134400 | bytes 8931328 | tf_op jit(solution)/shard_map/dot_general | solution.py:537
  71.5 6.2 %convolution_convert_fusion.3 = bf16[512,512]{1,0:T(8,128)(2,1)S(1)} fusion(bf16[512,4096]{1,0:T(8,128)(2,1)} %cot_hbm.1, bf16[512,4096]{1,0:T(8,128)(2,1)} %param.18), kind=kOutput, calls=%fused_computation.44 | convolution fusion | flops 2147745792 | bytes 8912896 | tf_op jit(solution)/shard_map/dot_general | solution.py:547
  79.0 15.1 %all-gather.2.cloned.1.call-done = bf16[8,16,16,1024]{3,2,1,0:T(8,128)(2,1)} async-done(((bf16[1,16,16,1024]{3,2,1,0:T(8,128)(2,1)}), bf16[8,16,16,1024]{3,2,1,0:T(8,128)(2,1)}) %all-gather.2.cloned.1.call-update) | async-done | bytes 4194320 | tf_op jit(solution)/shard_map/all_gather | solution.py:534
  94.2 4.5 %convolution_convert_fusion.2 = bf16[2048,512]{1,0:T(8,128)(2,1)S(1)} fusion(bf16[2048,1024]{1,0:T(8,128)(2,1)} %bitcast.99, bf16[1024,512]{1,0:T(8,128)(2,1)S(1)} %copy-done.3), kind=kOutput, calls=%fused_computation.13 | convolution fusion | flops 2148532224 | bytes 7340032 | tf_op jit(solution)/shard_map/dot_general | solution.py:540
  100.2 2.5 %reshape.261 = bf16[8,256,4,128]{3,2,1,0:T(4,128)(2,1)S(1)} reshape(bf16[8,8,32,512]{3,2,1,0:T(8,128)(2,1)} %bitcast.91) | data formatting | bytes 4194304 | tf_op jit(solution)/shard_map/reshape | solution.py:102
  102.7 4.8 %convolution_convert_fusion.1 = bf16[2048,512]{1,0:T(8,128)(2,1)S(1)} fusion(bf16[2048,1024]{1,0:T(8,128)(2,1)} %bitcast.100, bf16[1024,512]{1,0:T(8,128)(2,1)} %wk_hbm.1), kind=kOutput, calls=%fused_computation.12 | convolution fusion | flops 2148532224 | bytes 7340032 | tf_op jit(solution)/shard_map/dot_general | solution.py:539
  109.0 4.0 %reshape.264 = bf16[8,256,4,128]{3,2,1,0:T(4,128)(2,1)} reshape(bf16[8,8,32,512]{3,2,1,0:T(8,128)(2,1)} %bitcast.92) | data formatting | bytes 4194304 | tf_op jit(solution)/shard_map/reshape | solution.py:102
  113.0 2.6 %fusion.22 = (f32[8,4,64]{2,1,0:T(4,128)S(1)}, f32[8,4,64,256]{3,2,1,0:T(8,128)S(1)}) fusion(bf16[8,256,4,128]{3,2,1,0:T(4,128)(2,1)} %reshape.264, bf16[8,64,4,128]{3,2,1,0:T(4,128)(2,1)S(1)} %reshape.262), kind=kOutput, calls=%fused_computation.32 | convolution fusion | flops 135788544 | bytes 4726784 | tf_op jit(solution)/shard_map/bqhd,bkhd->bhqk/dot_general | solution.py:28
  118.8 2.4 %convert_bitcast_fusion = bf16[8,256,4,128]{1,3,2,0:T(8,128)(2,1)} fusion(bf16[8,64,4,128]{3,2,1,0:T(4,128)(2,1)S(1)} %reshape.266, f32[8,4,64,256]{3,2,1,0:T(8,128)S(1)} %get-tuple-element.20, f32[8,4,64]{2,1,0:T(4,128)S(1)} %get-tuple-element.19), kind=kOutput, calls=%fused_computation.20 | convolution fusion | flops 137363456 | bytes 4726784 | tf_op jit(solution)/shard_map/bhqk,bqhd->bkhd/dot_general | solution.py:50
  122.4 16.3 %convert_bitcast_fusion.1 = bf16[8,256,4,128]{1,3,2,0:T(8,128)(2,1)} fusion(f32[8,4,64,256]{3,2,1,0:T(8,128)} %fusion.17, f32[8,4,64,256]{3,2,1,0:T(8,128)} %copy-done.8, bf16[8,64,4,128]{3,2,1,0:T(4,128)(2,1)S(1)} %reshape.262, f32[8,4,64]{2,1,0:T(4,128)S(1)} %get-tuple-element.19), kind=kOutput, calls=%fused_computation.21 | convolution fusion | flops 142608640 | bytes 6823936 | tf_op jit(solution)/shard_map/bhqk,bqhd->bkhd/dot_general | solution.py:47
  138.7 3.0 %copy.95 = bf16[8,256,4,128]{3,2,1,0:T(4,128)(2,1)S(1)} copy(bf16[8,256,4,128]{1,3,2,0:T(8,128)(2,1)} %convert_bitcast_fusion.1) | data formatting | bytes 4194304 | tf_op jit(solution)/shard_map/convert_element_type | solution.py:49
  141.7 2.3 reshape.267
  144.0 3.2 %copy.96 = bf16[8,8,32,512]{3,2,1,0:T(8,128)(2,1)} copy(bf16[8,8,32,512]{3,2,0,1:T(8,128)(2,1)} %bitcast.93) | data formatting | bytes 4194304 | tf_op jit(solution)/shard_map/transpose | solution.py:108
  147.2 3.0 %copy.98 = bf16[8,256,4,128]{3,2,1,0:T(4,128)(2,1)S(1)} copy(bf16[8,256,4,128]{1,3,2,0:T(8,128)(2,1)} %convert_bitcast_fusion) | data formatting | bytes 4194304 | tf_op jit(solution)/shard_map/convert_element_type | solution.py:52
  150.2 2.3 reshape.269
  152.4 3.2 %copy.99 = bf16[8,8,32,512]{3,2,1,0:T(8,128)(2,1)} copy(bf16[8,8,32,512]{3,2,0,1:T(8,128)(2,1)} %bitcast.94) | data formatting | bytes 4194304 | tf_op jit(solution)/shard_map/transpose | solution.py:108
  155.6 68.9 %shard_map.147 = (bf16[2,128,1024]{2,1,0:T(8,128)(2,1)}, bf16[512,256]{1,0:T(8,128)(2,1)}, bf16[64,512]{1,0:T(8,128)(2,1)}, bf16[64,512]{1,0:T(8,128)(2,1)}) custom-call(s32[32]{0:T(128)} %select_reduce_fusion.position_ref, s32[16]{0:T(128)} %multiply_reduce_fusion.2.column_ref, bf16[512,512]{1,0:T(8,128)(2,1)} %bitcast.102, bf16[512,4096]{1,0:T(8,128)(2,1)} %cot_hbm.1, ...), custom_call_target="tpu_custom_call" | custom-call | tf_op jit(solution)/shard_map/pallas_call | solution.py:464
  (71 shorter events, 26.6 us)
Async XLA Ops:
  17.5 2.2 copy-start
  17.5 2.6 %copy-start.2 = (bf16[1024,1024]{1,0:T(8,128)(2,1)S(1)}, bf16[1024,1024]{1,0:T(8,128)(2,1)}, u32[]{:S(2)}) copy-start(bf16[1024,1024]{1,0:T(8,128)(2,1)} %param.23) | copy-start | bytes 6291460
  20.0 8.4 %copy-start.6 = (s32[128,2]{0,1:T(2,128)S(1)}, s32[128,2]{0,1:T(2,128)}, u32[]{:S(2)}) copy-start(s32[128,2]{0,1:T(2,128)} %param.15) | copy-start | bytes 3076
  21.6 16.1 %all-to-all-start = ((bf16[8,2,16,1024]{3,2,1,0:T(8,128)(2,1)}), bf16[8,2,16,1024]{3,2,1,0:T(8,128)(2,1)S(1)}, u32[]{:S(2)}, u32[]{:S(2)}) async-start(bf16[8,2,16,1024]{3,2,1,0:T(8,128)(2,1)} %bitcast.87), calls=%async_computation | async-start | bytes 1048576 | tf_op jit(solution)/shard_map/all_to_all | solution.py:529
  39.5 22.2 %all-to-all-start.1 = ((bf16[32,16,1024]{2,1,0:T(8,128)(2,1)}), bf16[32,16,1024]{2,1,0:T(8,128)(2,1)S(1)}, u32[]{:S(2)}, u32[]{:S(2)}) async-start(bf16[32,16,1024]{2,1,0:T(8,128)(2,1)} %broadcast_select_fusion), calls=%async_computation.1 | async-start | bytes 2097152 | tf_op jit(solution)/shard_map/all_to_all | solution.py:532
  46.3 47.9 %all-gather.2.cloned.1.call-start = ((), (), s32[]{:S(2)}) async-start(), calls=%async_computation.2 | async-start | bytes 4718592 | tf_op jit(solution)/shard_map/all_gather | solution.py:534
  62.3 4.2 %copy-start.7 = (f32[4096]{0:T(1024)S(1)}, f32[4096]{0:T(1024)}, u32[]{:S(2)}) copy-start(f32[4096]{0:T(1024)} %param.16) | copy-start | bytes 49156
  63.3 3.5 %copy-start.1 = (bf16[512,4096]{1,0:T(8,128)(2,1)S(1)}, bf16[512,4096]{1,0:T(8,128)(2,1)}, u32[]{:S(2)}) copy-start(bf16[512,4096]{1,0:T(8,128)(2,1)} %param.12) | copy-start | bytes 12582916
  71.4 22.7 %copy-start.3 = (bf16[1024,512]{1,0:T(8,128)(2,1)S(1)}, bf16[1024,512]{1,0:T(8,128)(2,1)}, u32[]{:S(2)}) copy-start(bf16[1024,512]{1,0:T(8,128)(2,1)} %wv_hbm.1) | copy-start | bytes 3145732
  115.6 3.1 %copy-start.8 = (f32[8,4,64,256]{3,2,1,0:T(8,128)}, f32[8,4,64,256]{3,2,1,0:T(8,128)S(1)}, u32[]{:S(2)}) copy-start(f32[8,4,64,256]{3,2,1,0:T(8,128)S(1)} %get-tuple-element.20) | copy-start | bytes 6291460
  224.5 4.0 %copy-start.5 = (bf16[64,512]{1,0:T(8,128)(2,1)S(1)}, bf16[64,512]{1,0:T(8,128)(2,1)}, u32[]{:S(2)}) copy-start(bf16[64,512]{1,0:T(8,128)(2,1)} %get-tuple-element.10) | copy-start | bytes 196612
  224.5 4.6 %copy-start.4 = (bf16[64,512]{1,0:T(8,128)(2,1)S(1)}, bf16[64,512]{1,0:T(8,128)(2,1)}, u32[]{:S(2)}) copy-start(bf16[64,512]{1,0:T(8,128)(2,1)} %get-tuple-element.11) | copy-start | bytes 196612
Sparse Core Ops, SparseCore 0:
  63.4 30.7 all-gather.1

commit v3 on v2

--- a/solution.py
+++ b/solution.py
@@ -36,21 +36,6 @@
         "bhqk,bkhd->bqhd", probs_low, values_all, preferred_element_type=jnp.float32
     ).astype(jnp.bfloat16)
     return (raw_scores, probs_full, probs_low, mixed)
-
-
-def attention_grads(queries, values_all, raw_scores, probs_full, probs_low, d_mixed):
-    head_width = queries.shape[-1]
-    d_probs = jnp.einsum("bqhd,bkhd->bhqk", d_mixed, values_all, preferred_element_type=jnp.float32)
-    d_capped = probs_full * (d_probs - jnp.sum(probs_full * d_probs, axis=-1, keepdims=True))
-    slope = jnp.tanh(raw_scores / SOFTCAP)
-    d_raw = (d_capped * (1.0 - slope * slope) * head_width ** (-0.5)).astype(jnp.bfloat16)
-    d_keys = jnp.einsum(
-        "bhqk,bqhd->bkhd", d_raw, queries, preferred_element_type=jnp.float32
-    ).astype(jnp.bfloat16)
-    d_values = jnp.einsum(
-        "bhqk,bqhd->bkhd", probs_low, d_mixed, preferred_element_type=jnp.float32
-    ).astype(jnp.bfloat16)
-    return (d_keys, d_values)
 
 
 def encode(nbr_embed, enc_gain, enc_qkv, enc_out):
@@ -93,19 +78,6 @@
     receive_match = (receive_position[:, None] == buffer_ids[None, :]).astype(jnp.int32)
     position_slot = jnp.sum(receive_match * column_ids[:, None], axis=0)
     return (send_column, column_position, receive_position, position_slot)
-
-
-def to_blocks(rows, enc_count, block_count, head_count):
-    features = rows.shape[1]
-    keys = rows.shape[0] // block_count
-    rows = rows.reshape(enc_count, block_count, keys // enc_count, features)
-    return rows.transpose(1, 0, 2, 3).reshape(block_count, keys, head_count, features // head_count)
-
-
-def from_blocks(blocks, enc_count):
-    block_count, keys, head_count, head_width = blocks.shape
-    rows = blocks.reshape(block_count, enc_count, keys // enc_count, head_count * head_width)
-    return rows.transpose(1, 0, 2, 3).reshape(block_count * keys, head_count * head_width)
 
 
 def neighbours():
@@ -495,6 +467,273 @@
     )(position, column, *operands)
 
 
+def project_queries(hidden, gain, wq, normed, out):
+    def norm(i, carry):
+        at = pl.ds(pl.multiple_of(i * 16, 16), 16)
+        wide = hidden[at, :].astype(jnp.float32)
+        factor = lax.rsqrt(jnp.mean(wide * wide, axis=-1, keepdims=True) + EPSILON)
+        normed[at, :] = (wide * factor * gain[...]).astype(jnp.bfloat16)
+        return carry
+
+    lax.fori_loop(0, hidden.shape[0] // 16, norm, 0)
+
+    def tile(i, carry):
+        at = pl.ds(pl.multiple_of(i * 256, 256), 256)
+        out[at, :] = jnp.dot(normed[at, :], wq[...], preferred_element_type=jnp.float32).astype(jnp.bfloat16)
+        return carry
+
+    lax.fori_loop(0, hidden.shape[0] // 256, tile, 0)
+
+
+def project_cotangents(cot, wo, out):
+    def tile(i, carry):
+        at = pl.ds(pl.multiple_of(i * 256, 256), 256)
+        out[at, :] = lax.dot_general(
+            cot[at, :], wo[...], (((1,), (1,)), ((), ())), preferred_element_type=jnp.float32
+        ).astype(jnp.bfloat16)
+        return carry
+
+    lax.fori_loop(0, cot.shape[0] // 256, tile, 0)
+
+
+def front_kernel(
+    send_ref, receive_ref,
+    encoded, gain, hidden_hbm, cot_hbm, wq_hbm, wo_hbm, wk_hbm, wv_hbm,
+    q_out, dm_out, k_out, v_out, rows_out,
+    hidden, cot, wq, wo, wk, wv, normed, columns, outgoing, incoming, rows,
+    load_sems, s_enc, s_gen, s_ring, s_core, rows_sems,
+):
+    loads = []
+    for number, (src, dst) in enumerate(
+        ((hidden_hbm, hidden), (wq_hbm, wq), (cot_hbm, cot), (wo_hbm, wo), (wk_hbm, wk), (wv_hbm, wv))
+    ):
+        copy = pltpu.make_async_copy(src, dst, load_sems.at[number])
+        copy.start()
+        loads.append(copy)
+    enc, gen, where, at = neighbours()
+    z, core = where["z"], where["core"]
+    entry_barrier(enc, gen)
+
+    def enc_copy(step):
+        peer = (enc + step) % 8
+        return send(
+            encoded.at[:, pl.ds(pl.multiple_of(peer * 16, 16), 16), :],
+            columns.at[pl.ds(enc * 2, 2)],
+            s_enc,
+            step - 1,
+            (peer, gen),
+        )
+
+    def start_enc(step, carry):
+        enc_copy(step).start()
+        return carry
+
+    lax.fori_loop(1, 8, start_enc, 0)
+    columns[pl.ds(enc * 2, 2)] = encoded[:, pl.ds(pl.multiple_of(enc * 16, 16), 16), :]
+
+    loads[0].wait()
+    loads[1].wait()
+    project_queries(hidden, gain, wq, normed, q_out)
+
+    def wait_enc(step, carry):
+        enc_copy(step).wait_recv()
+        return carry
+
+    lax.fori_loop(1, 8, wait_enc, 0)
+    for j in range(32):
+        outgoing[j] = columns[send_ref[j]]
+
+    def gen_copy(step):
+        peer = (gen + step) % 16
+        return send(
+            outgoing.at[pl.ds(peer * 2, 2)], incoming.at[pl.ds(gen * 2, 2)], s_gen, step - 1, (enc, peer)
+        )
+
+    def start_gen(step, carry):
+        gen_copy(step).start()
+        return carry
+
+    lax.fori_loop(1, 16, start_gen, 0)
+    incoming[pl.ds(gen * 2, 2)] = outgoing[pl.ds(gen * 2, 2)]
+    loads[2].wait()
+    loads[3].wait()
+    project_cotangents(cot, wo, dm_out)
+
+    def wait_gen(step, carry):
+        gen_copy(step).wait_recv()
+        return carry
+
+    lax.fori_loop(1, 16, wait_gen, 0)
+    for j in range(16):
+        rows[enc, j * 16 : j * 16 + 16, :] = incoming[receive_ref[j]]
+
+    minus, plus, across = (z + 3) % 4 * 2 + core, (z + 1) % 4 * 2 + core, (z + 2) % 4 * 2 + core
+    first, second = pl.ds(0, 128), pl.ds(128, 128)
+
+    def share(ref, sems, number, device):
+        return send(ref, ref, sems, number, device)
+
+    up, down, peer = at("z", 1), at("z", 3), at("core", 1)
+    ring = [
+        share(rows.at[enc], s_ring, 0, up),
+        share(rows.at[enc], s_ring, 1, down),
+        share(rows.at[minus, first], s_ring, 2, up),
+        share(rows.at[plus, second], s_ring, 3, down),
+    ]
+    cross = [
+        share(rows.at[enc], s_core, 0, peer),
+        share(rows.at[minus], s_core, 1, peer),
+        share(rows.at[plus], s_core, 2, peer),
+        share(rows.at[across, first], s_core, 3, peer),
+        share(rows.at[across, second], s_core, 4, peer),
+    ]
+    ring[0].start()
+    ring[1].start()
+    cross[0].start()
+    loads[4].wait()
+    loads[5].wait()
+
+    def project(piece):
+        k_out[piece] = jnp.dot(rows[piece], wk[...], preferred_element_type=jnp.float32).astype(jnp.bfloat16)
+        v_out[piece] = jnp.dot(rows[piece], wv[...], preferred_element_type=jnp.float32).astype(jnp.bfloat16)
+
+    def of_peer(piece):
+        return piece + 1 - 2 * core
+
+    project(enc)
+    ring[0].wait_recv()
+    ring[2].start()
+    cross[1].start()
+    ring[1].wait_recv()
+    ring[3].start()
+    cross[2].start()
+    cross[0].wait_recv()
+
+    def project_some(pieces):
+        def body(i, carry):
+            piece = pieces[0]
+            for number in range(1, len(pieces)):
+                piece = jnp.where(i == number, pieces[number], piece)
+            project(piece)
+            return carry
+
+        lax.fori_loop(0, len(pieces), body, 0)
+
+    project_some((of_peer(enc), minus, plus))
+    ring[2].wait_recv()
+    cross[3].start()
+    ring[3].wait_recv()
+    cross[4].start()
+    cross[1].wait_recv()
+    cross[2].wait_recv()
+    project_some((across, of_peer(minus), of_peer(plus)))
+    cross[3].wait_recv()
+    cross[4].wait_recv()
+    keep = pltpu.make_async_copy(rows, rows_out, rows_sems.at[0])
+    keep.start()
+    project(of_peer(across))
+    keep.wait()
+
+    def drain_gen(step, carry):
+        gen_copy(step).wait_send()
+        return carry
+
+    def drain_enc(step, carry):
+        enc_copy(step).wait_send()
+        return carry
+
+    lax.fori_loop(1, 16, drain_gen, 0)
+    lax.fori_loop(1, 8, drain_enc, 0)
+    for copy in ring + cross:
+        copy.wait_send()
+
+
+def front(send_column, receive_position, encoded, gain, hidden, cot, wq, wo, wk, wv):
+    low = jnp.bfloat16
+    anywhere = pl.BlockSpec(memory_space=pl.ANY)
+    scalars = pl.BlockSpec(memory_space=pltpu.SMEM)
+    whole = pl.BlockSpec(memory_space=pltpu.VMEM)
+    operands = (hidden, cot, wq, wo, wk, wv)
+    return pl.pallas_call(
+        front_kernel,
+        out_shape=(
+            jax.ShapeDtypeStruct((512, 512), low),
+            jax.ShapeDtypeStruct((512, 512), low),
+            jax.ShapeDtypeStruct((8, 256, 512), low),
+            jax.ShapeDtypeStruct((8, 256, 512), low),
+            jax.ShapeDtypeStruct((8, 256, 1024), low),
+        ),
+        in_specs=[scalars] * 2 + [whole] * 2 + [anywhere] * 6,
+        out_specs=(whole,) * 4 + (anywhere,),
+        scratch_shapes=[pltpu.VMEM(a.shape, low) for a in operands]
+        + [
+            pltpu.VMEM((512, 4096), low),
+            pltpu.VMEM((16, 16, 1024), low),
+            pltpu.VMEM((32, 16, 1024), low),
+            pltpu.VMEM((32, 16, 1024), low),
+            pltpu.VMEM((8, 256, 1024), low),
+            pltpu.SemaphoreType.DMA((6,)),
+            pltpu.SemaphoreType.DMA((2, 7)),
+            pltpu.SemaphoreType.DMA((2, 15)),
+            pltpu.SemaphoreType.DMA((2, 4)),
+            pltpu.SemaphoreType.DMA((2, 5)),
+            pltpu.SemaphoreType.DMA((1,)),
+        ],
+        compiler_params=pltpu.CompilerParams(
+            collective_id=2, has_side_effects=True, vmem_limit_bytes=44 * 1024 * 1024
+        ),
+    )(send_column, receive_position, encoded, gain.reshape(1, -1), *operands)
+
+
+def attention_block(b, h, q_ref, dm_ref, k_ref, v_ref, mixed_ref, dk_ref, dv_ref):
+    width = 128
+    lanes = slice(h * width, h * width + width)
+    tokens = pl.ds(pl.multiple_of(b * CH, CH), CH)
+    keys = pl.ds(pl.multiple_of(b * 32, 32), 32)
+    scale = width ** (-0.5)
+    q, dm = q_ref[tokens, lanes], dm_ref[tokens, lanes]
+    k, v = k_ref[:, keys, lanes].reshape(256, width), v_ref[:, keys, lanes].reshape(256, width)
+    across = (((1,), (1,)), ((), ()))
+    raw = lax.dot_general(q, k, across, preferred_element_type=jnp.float32)
+    slope = jnp.tanh(raw * (scale / SOFTCAP))
+    expo = jnp.exp(SOFTCAP * slope)
+    probs = expo / jnp.sum(expo, axis=-1, keepdims=True)
+    low = probs.astype(jnp.bfloat16)
+    mixed_ref[tokens, lanes] = jnp.dot(low, v, preferred_element_type=jnp.float32).astype(jnp.bfloat16)
+    d_probs = lax.dot_general(dm, v, across, preferred_element_type=jnp.float32)
+    d_capped = probs * (d_probs - jnp.sum(probs * d_probs, axis=-1, keepdims=True))
+    d_raw = (d_capped * (1.0 - slope * slope) * scale).astype(jnp.bfloat16)
+    down = (((0,), (0,)), ((), ()))
+    d_keys = lax.dot_general(d_raw, q, down, preferred_element_type=jnp.float32)
+    d_values = lax.dot_general(low, dm, down, preferred_element_type=jnp.float32)
+    dk_ref[:, keys, lanes] = d_keys.astype(jnp.bfloat16).reshape(8, 32, width)
+    dv_ref[:, keys, lanes] = d_values.astype(jnp.bfloat16).reshape(8, 32, width)
+
+
+def attention_kernel(*refs):
+    def block(b, carry):
+        for h in range(4):
+            attention_block(b, h, *refs)
+        return carry
+
+    lax.fori_loop(0, 8, block, 0)
+
+
+def attention(q, dm, k, v):
+    whole = pl.BlockSpec(memory_space=pltpu.VMEM)
+    return pl.pallas_call(
+        attention_kernel,
+        out_shape=(
+            jax.ShapeDtypeStruct(q.shape, q.dtype),
+            jax.ShapeDtypeStruct(k.shape, k.dtype),
+            jax.ShapeDtypeStruct(v.shape, v.dtype),
+        ),
+        in_specs=[whole] * 4,
+        out_specs=(whole,) * 3,
+        compiler_params=pltpu.CompilerParams(vmem_limit_bytes=24 * 1024 * 1024),
+    )(q, dm, k, v)
+
+
 def local(
     hidden_states,
     grad_out,
@@ -515,54 +754,31 @@
     per_device, length, enc_width = nbr_embed.shape
     row_size = per_device * enc_count
     capacity = max(2, 2 * row_size // gen_count)
-    token_count, model_width = hidden_states.shape
-    head_feats = w_query.shape[1]
-    head_width = model_width // H
-    head_count = head_feats // head_width
-    block_count = token_count // CH
     send_column, column_position, receive_position, position_slot = routing(
         nbr_index, row_index, gen_count, per_device, row_size, capacity
     )
-    chunk = length // enc_count
     encoded = encode(nbr_embed, enc_gain, enc_qkv, enc_out)
-    pieces = encoded.reshape(per_device, enc_count, chunk, enc_width).transpose(1, 0, 2, 3)
-    columns = lax.all_to_all(pieces, "enc", split_axis=0, concat_axis=0, tiled=True)
-    columns = columns.reshape(row_size, chunk, enc_width)
-    outgoing = jnp.take(columns, send_column, axis=0)
-    incoming = lax.all_to_all(outgoing, "gen", split_axis=0, concat_axis=0, tiled=True)
-    slot_pieces = jnp.take(incoming, receive_position, axis=0)
-    slot_encoded = lax.all_gather(slot_pieces, "enc", axis=0, tiled=False)
-    slot_rows = slot_encoded.reshape(row_size * length, enc_width)
-    normed = rms_scale(hidden_states, gain)
-    queries = jnp.dot(normed, w_query, preferred_element_type=jnp.float32).astype(jnp.bfloat16)
-    queries = queries.reshape(block_count, CH, head_count, head_width)
-    keys_all = jnp.dot(slot_rows, w_key, preferred_element_type=jnp.float32).astype(jnp.bfloat16)
-    values_all = jnp.dot(slot_rows, w_value, preferred_element_type=jnp.float32).astype(
-        jnp.bfloat16
+    queries, d_mixed, keys_all, values_all, slot_rows = front(
+        send_column,
+        receive_position,
+        encoded,
+        gain,
+        hidden_states,
+        grad_out,
+        w_query,
+        w_out,
+        w_key,
+        w_value,
     )
-    keys_all = to_blocks(keys_all, enc_count, block_count, head_count)
-    values_all = to_blocks(values_all, enc_count, block_count, head_count)
-    raw_scores, probs_full, probs_low, mixed = attention_parts(queries, keys_all, values_all)
-    mixed_rows = mixed.reshape(token_count, head_feats)
-    d_mixed = jnp.dot(grad_out, w_out.T, preferred_element_type=jnp.float32).astype(jnp.bfloat16)
-    d_keys, d_values = attention_grads(
-        queries,
-        values_all,
-        raw_scores,
-        probs_full,
-        probs_low,
-        d_mixed.reshape(block_count, CH, head_count, head_width),
-    )
-    d_keys_rows = from_blocks(d_keys, enc_count)
-    d_values_rows = from_blocks(d_values, enc_count)
+    mixed, d_keys, d_values = attention(queries, d_mixed, keys_all, values_all)
     outputs = back(
         position_slot,
         column_position,
-        mixed_rows,
+        mixed,
         grad_out,
-        slot_rows,
-        d_keys_rows,
-        d_values_rows,
+        slot_rows.reshape(row_size * length, enc_width),
+        d_keys.reshape(row_size * length, -1),
+        d_values.reshape(row_size * length, -1),
         w_key,
         w_value,
     )

time: 238 us -> 171 us (0.72)
  Pallas kernels: 68.9 us -> 144 us
  matrix products: 53.6 us -> 9.01 us
  waiting for transfers between devices: 38.4 us -> 0 us
  local copies, waits for them, and re-layouts: 32.7 us -> 7.21 us
  starting transfers between devices: 13.8 us -> 0 us
  between operations: 14.3 us -> 0.83 us
  other arithmetic: 15 us -> 9.4 us
    pallas_call x0 -> x2, Pallas kernels: none -> 70.5 us  [the longest x1 55.3 us: front(): pl.pallas_call(front_kernel, out_shape=(jax.ShapeDtypeStruct((512, 512),...]
    dot_general x7 -> x0, matrix products: 41 us -> none  [the longest x1 16.3 us: attention_grads(): jnp.einsum('bhqk,bqhd->bkhd', d_raw, queries, preferred_element_type=jnp....]
    all_to_all x2 -> x0, waiting for transfers between devices: 23.2 us -> none  [the longest x1 15.1 us: local(): lax.all_to_all(outgoing, 'gen', split_axis=0, concat_axis=0, tiled=True)]
    all_gather x1 -> x0, waiting for transfers between devices: 15.1 us -> none  [local(): slot_encoded = lax.all_gather(slot_pieces, 'enc', axis=0, tiled=False)]
    reshape x9 -> x0, local copies, waits for them, and re-layouts: 15.1 us -> none  [the longest x2 6.53 us: to_blocks(): rows.transpose(1, 0, 2, 3)]
    all_to_all x2 -> x0, starting transfers between devices: 13.6 us -> none  [the longest x1 6.8 us: local(): lax.all_to_all(pieces, 'enc', split_axis=0, concat_axis=0, tiled=True)]
    convert_element_type x3 -> x0, local copies, waits for them, and re-layouts: 6.39 us -> none  [the longest x1 2.99 us: attention_grads(): d_keys = jnp.einsum('bhqk,bqhd->bkhd', d_raw, queries, preferred_element_...]
    transpose x2 -> x0, local copies, waits for them, and re-layouts: 6.35 us -> none  [from_blocks(): rows.transpose(1, 0, 2, 3)]
  transfers between devices with their start and end apart: 3 -> 0, of which waited for: 3 -> 0; matrix products, arithmetic and copies ran while one was open for 7% -> 0% of each run, Pallas kernels for 0% -> 0%
where the time goes in v3:
time: 171 us; the launch traced here: 170 us
  Pallas kernels  144 us (84%)
  other arithmetic  9.4 us (5%)
  matrix products  9.01 us (5%)
  local copies, waits for them, and re-layouts  7.21 us (4%)
    pallas_call x1, Pallas kernels, back(): pl.pallas_call(back_kernel, out_shape=(jax.ShapeDtypeStruct((2, 128, 1024...  73.4 us
    pallas_call x1, Pallas kernels, front(): pl.pallas_call(front_kernel, out_shape=(jax.ShapeDtypeStruct((512, 512),...  55.3 us
    pallas_call x1, Pallas kernels, attention(): pl.pallas_call(attention_kernel, out_shape=(jax.ShapeDtypeStruct(q.shape,...  15.2 us
    unnamed x24, local copies, waits for them, and re-layouts  6.53 us
    convert_element_type x4, other arithmetic, local(): return tuple((output.astype(jnp.float32) for output in outputs))  6 us
    dot_general x1, matrix products, encode(): jnp.dot(normed, enc_qkv, preferred_element_type=jnp.float32)  4.61 us

profile of v3, /device:TPU:1, one launch (start us, length us, event | category | flops | bytes accessed | tf_op | source)
XLA Modules:
  0.0 170.4 jit_solution(13551915289994137866)
XLA Ops:
  0.7 1.3 fusion.11
  1.9 0.8 copy.30
  3.2 0.2 fusion.17
  3.9 0.6 multiply_reduce_fusion.1.column_ref
  4.5 0.6 select_reduce_fusion.position_ref
  5.3 4.6 %fusion.2 = bf16[32,8,24,128]{3,1,2,0:T(8,128)(2,1)S(1)} fusion(bf16[256,1024]{1,0:T(8,128)(2,1)S(1)} %bitcast.57, bf16[1024,3072]{1,0:T(8,128)(2,1)} %param.22), kind=kOutput, calls=%fused_computation.6 | convolution fusion | flops 1611399168 | bytes 8388608 | tf_op jit(solution)/shard_map/dot_general | solution.py:44
  10.0 0.3 copy.44
  10.3 0.3 fusion.31
  10.6 1.1 copy.41
  11.7 1.5 fusion.5
  13.2 2.2 %convolution_convert_fusion.1 = bf16[2,8,128,128]{3,2,1,0:T(8,128)(2,1)S(1)} fusion(f32[2,8,128,128]{2,3,1,0:T(8,128)} %fusion.5, bf16[2,128,1,8,128]{1,4,3,0,2:T(8,128)(2,1)} %copy.41), kind=kOutput, calls=%fused_computation.12 | convolution fusion | flops 67897472 | bytes 2097152 | tf_op jit(solution)/shard_map/bhqk,bkhd->bqhd/dot_general | solution.py:35
  15.5 0.7 fusion.8.encoded
  16.3 0.4 copy-done
  16.6 0.3 copy-done.1
  16.9 55.3 %shard_map.147 = (bf16[512,512]{1,0:T(8,128)(2,1)S(1)}, bf16[512,512]{1,0:T(8,128)(2,1)S(1)}, bf16[8,256,512]{2,1,0:T(8,128)(2,1)S(1)}, bf16[8,256,512]{2,1,0:T(8,128)(2,1)S(1)}, bf16[8,256,1024]{2,1,0:T(8,128)(2,1)}) custom-call(s32[32]{0:T(128)S(1)} %multiply_reduce_fusion.send_ref, s32[16]{0:T(128)S(1)} %dynamic-slice_add_fusion.receive_ref, ...), custom_call_target="tpu_custom_call" | custom-call | tf_op jit(solution)/shard_map/pallas_call | solution.py:657
  72.2 15.2 %shard_map.148 = (bf16[512,512]{1,0:T(8,128)(2,1)S(1)}, bf16[8,256,512]{2,1,0:T(8,128)(2,1)S(1)}, bf16[8,256,512]{2,1,0:T(8,128)(2,1)S(1)}) custom-call(bf16[512,512]{1,0:T(8,128)(2,1)S(1)} %get-tuple-element.16.refs_0_, bf16[512,512]{1,0:T(8,128)(2,1)S(1)} %get-tuple-element.17.refs_1_, bf16[8,256,512]{2,1,0:T(8,128)(2,1)S(1)} %get-tuple-element.18.refs_2_, ...), custom_call_target="tpu_custom_call" | custom-call | tf_op jit(solution)/shard_map/pallas_call | solution.py:724
  87.5 1.3 copy-done.2
  88.8 1.3 copy-done.3
  90.2 0.8 copy-done.4
  91.0 73.4 %shard_map.149 = (bf16[2,128,1024]{2,1,0:T(8,128)(2,1)}, bf16[512,256]{1,0:T(8,128)(2,1)}, bf16[64,512]{1,0:T(8,128)(2,1)}, bf16[64,512]{1,0:T(8,128)(2,1)}) custom-call(s32[32]{0:T(128)} %select_reduce_fusion.position_ref, s32[16]{0:T(128)} %multiply_reduce_fusion.1.column_ref, bf16[512,512]{1,0:T(8,128)(2,1)} %copy-done.4, bf16[512,4096]{1,0:T(8,128)(2,1)} %cot_hbm.3, ...), custom_call_target="tpu_custom_call" | custom-call | tf_op jit(solution)/shard_map/pallas_call | solution.py:436
  164.4 1.5 convert_element_type.63
  166.0 1.5 convert_element_type.64
  167.5 2.1 %convert_element_type.61 = f32[2,128,1024]{2,1,0:T(8,128)} convert(bf16[2,128,1024]{2,1,0:T(8,128)(2,1)} %get-tuple-element.24) | non-fusion elementwise | flops 262144 | bytes 1572864 | tf_op jit(solution)/shard_map/convert_element_type | solution.py:785
  169.6 0.8 convert_element_type.62
  (33 shorter events, 1.3 us)
Async XLA Ops:
  0.6 4.5 %copy-start.6 = (bf16[2,128,1024]{2,1,0:T(8,128)(2,1)S(1)}, bf16[2,128,1024]{2,1,0:T(8,128)(2,1)}, u32[]{:S(2)}) copy-start(bf16[2,128,1024]{2,1,0:T(8,128)(2,1)} %param.14) | copy-start | bytes 1572868
  0.6 4.5 %copy-start.9 = (f32[1024]{0:T(1024)S(1)}, f32[1024]{0:T(1024)}, u32[]{:S(2)}) copy-start(f32[1024]{0:T(1024)} %param.21) | copy-start | bytes 12292
  13.2 2.4 %copy-start.7 = (bf16[1024,1024]{1,0:T(8,128)(2,1)S(1)}, bf16[1024,1024]{1,0:T(8,128)(2,1)}, u32[]{:S(2)}) copy-start(bf16[1024,1024]{1,0:T(8,128)(2,1)} %param.23) | copy-start | bytes 6291460
  15.4 1.3 copy-start
  15.4 1.6 copy-start.1
  15.4 1.6 copy-start.5
  87.5 1.3 copy-start.2
  88.8 1.3 copy-start.3
  90.2 0.8 copy-start.4
  164.4 5.2 %copy-start.8 = (bf16[512,256]{1,0:T(8,128)(2,1)S(1)}, bf16[512,256]{1,0:T(8,128)(2,1)}, u32[]{:S(2)}) copy-start(bf16[512,256]{1,0:T(8,128)(2,1)} %get-tuple-element.25) | copy-start | bytes 786436

commit v4 on v0

v4 whole, which is shorter than its diff:
```python
import functools
import types

import jax
import jax.numpy as jnp
from jax import lax
from jax.experimental import pallas as pl
from jax.experimental.pallas import tpu as pltpu
from jax.sharding import PartitionSpec as P

EH = 8
CH = 64
SOFTCAP = 5.0
EPSILON = 1e-06
MESH = pl.DeviceIdType.MESH


def neighbours():
    enc, gen = lax.axis_index("enc"), lax.axis_index("gen")
    z, core, x, y = enc // 2, enc % 2, gen // 4, gen % 4

    def at(axis, step):
        if axis == "x":
            return (enc, (x + step) % 4 * 4 + y)
        if axis == "y":
            return (enc, x * 4 + (y + step) % 4)
        if axis == "z":
            return ((z + step) % 4 * 2 + core, gen)
        return (z * 2 + (1 - core), gen)

    return enc, gen, {"x": x, "y": y, "z": z, "core": core}, at


def send(src, dst, sems, number, device):
    return pltpu.make_async_remote_copy(
        src_ref=src,
        dst_ref=dst,
        send_sem=sems.at[0, number],
        recv_sem=sems.at[1, number],
        device_id=device,
        device_id_type=MESH,
    )


def add_rows(out, out_at, terms, rows, step):
    def body(i, carry):
        total = None
        for ref, at in terms:
            value = ref[pl.ds(pl.multiple_of(at + i * step, step), step), :].astype(jnp.float32)
            total = value if total is None else total + value
        if len(out.shape) == 3:
            out[out_at + i] = total.astype(out.dtype)
        else:
            out[pl.ds(pl.multiple_of(out_at + i * step, step), step), :] = total.astype(out.dtype)
        return carry

    lax.fori_loop(0, rows // step, body, 0)


class Ring:
    def __init__(self, src, buf, sems, axis, where, at):
        self.src, self.buf = src, buf
        self.rows = src.shape[0] // 4
        self.half = self.rows // 2
        self.me = where[axis]
        half = self.half
        self.plus, self.minus = (self.me + 1) % 4, (self.me + 3) % 4
        across = (self.me + 2) % 4
        pieces = (
            (across, 0, 1),
            (self.plus, 1, 1),
            (self.plus, 0, 1),
            (across, 1, 3),
            (self.minus, 0, 3),
            (self.minus, 1, 3),
        )
        self.copies = []
        for number, (chunk, side, step) in enumerate(pieces):
            start = pl.multiple_of(chunk * self.rows + side * half, half)
            self.copies.append(
                send(
                    src.at[pl.ds(start, half), :],
                    buf.at[pl.ds(number * half, half), :],
                    sems,
                    number,
                    at(axis, step),
                )
            )

    def first(self):
        self.copies[0].start()
        self.copies[3].start()

    def second(self):
        self.copies[1].start()
        self.copies[4].start()

    def third(self, step):
        half = self.half
        self.copies[0].wait_recv()
        start = self.plus * self.rows
        add_rows(self.src, start, ((self.src, start), (self.buf, 0)), half, step)
        self.copies[2].start()
        self.copies[3].wait_recv()
        start = self.minus * self.rows + half
        add_rows(self.src, start, ((self.src, start), (self.buf, 3 * half)), half, step)
        self.copies[5].start()

    def last(self, out, out_at, step):
        half = self.half
        for number in (1, 2, 4, 5):
            self.copies[number].wait_recv()
        start = self.me * self.rows
        add_rows(out, out_at, ((self.src, start), (self.buf, 2 * half), (self.buf, 4 * half)), half, step)
        add_rows(
            out, out_at + (half // step if len(out.shape) == 3 else half), ((self.src, start + half), (self.buf, half), (self.buf, 5 * half)), half, step
        )

    def drain(self):
        for copy in self.copies:
            copy.wait_send()


HALVES = 2
DOWN = (((0,), (0,)), ((), ()))
ACROSS = (((1,), (1,)), ((), ()))


def dot(a, b, dims=(((1,), (0,)), ((), ()))):
    return lax.dot_general(a, b, dims, preferred_element_type=jnp.float32)


def loop(low, high, body):
    def step(i, carry):
        body(i)
        return carry

    lax.fori_loop(low, high, step, 0)


def rows_of(start, size):
    return pl.ds(pl.multiple_of(start, size), size)


def normalise(values, gain, out):
    def body(i):
        at = rows_of(i * 16, 16)
        wide = values[at, :].astype(jnp.float32)
        factor = lax.rsqrt(jnp.mean(wide * wide, axis=-1, keepdims=True) + EPSILON)
        out[at, :] = (wide * factor * gain[...]).astype(jnp.bfloat16)

    loop(0, values.shape[0] // 16, body)


def softcapped(q, k):
    scale = q.shape[-1] ** (-0.5)
    slope = jnp.tanh(dot(q, k, ACROSS) * (scale / SOFTCAP))
    expo = jnp.exp(SOFTCAP * slope)
    return slope, expo / jnp.sum(expo, axis=-1, keepdims=True)


def encoder_attention(i, projected, attended):
    at = rows_of(i * 128, 128)
    for h in range(EH):
        q, k, v = (projected[at, part * 1024 + h * 128 : part * 1024 + h * 128 + 128] for part in range(3))
        _, probs = softcapped(q, k)
        attended[at, h * 128 : h * 128 + 128] = dot(probs.astype(jnp.bfloat16), v).astype(jnp.bfloat16)


def pair_refs(b, p, r):
    keys, rows = rows_of(b * 32, 32), rows_of((b * 2 + p) * 128, 128)
    k = r.kv[:, keys, p * 256 : p * 256 + 256].reshape(256, 256)
    v = r.kv[:, keys, 512 + p * 256 : 512 + p * 256 + 256].reshape(256, 256)
    return keys, rows, k, v


def pair_probs(k, q_pair):
    slope = jnp.tanh(dot(k, q_pair, ACROSS) * (128 ** (-0.5) / SOFTCAP))
    expo = jnp.exp(SOFTCAP * slope)
    return slope, expo * (1.0 / jnp.sum(expo, axis=0, keepdims=True))


def attention_forward(b, r, mixed):
    tokens = rows_of(b * CH, CH)
    for p in range(2):
        keys, rows, k, v = pair_refs(b, p, r)
        _, probs = pair_probs(k, r.q_pairs[rows, :])
        both = dot(probs.astype(jnp.bfloat16), v, DOWN).astype(jnp.bfloat16)
        mixed[tokens, p * 256 : p * 256 + 128] = both[0:64, 0:128]
        mixed[tokens, p * 256 + 128 : p * 256 + 256] = both[64:128, 128:256]


def attention_backward(b, r):
    for p in range(2):
        keys, rows, k, v = pair_refs(b, p, r)
        q_pair, dm_pair = r.q_pairs[rows, :], r.dm_pairs[rows, :]
        slope, probs = pair_probs(k, q_pair)
        d_probs = dot(v, dm_pair, ACROSS)
        d_capped = probs * (d_probs - jnp.sum(probs * d_probs, axis=0, keepdims=True))
        d_raw = (d_capped * (1.0 - slope * slope) * 128 ** (-0.5)).astype(jnp.bfloat16)
        d_keys = dot(d_raw, q_pair).astype(jnp.bfloat16)
        d_values = dot(probs.astype(jnp.bfloat16), dm_pair).astype(jnp.bfloat16)
        r.dkv[:, keys, p * 256 : p * 256 + 256] = d_keys.reshape(8, 32, 256)
        r.dkv[:, keys, 512 + p * 256 : 512 + p * 256 + 256] = d_values.reshape(8, 32, 256)


class Exchange:
    def __init__(self, count, copy):
        self.count, self.copy = count, copy

    def start(self):
        loop(1, self.count, lambda step: self.copy(step).start())

    def receive(self):
        loop(1, self.count, lambda step: self.copy(step).wait_recv())

    def drain(self):
        loop(1, self.count, lambda step: self.copy(step).wait_send())


def whole_kernel(tree, *refs):
    r = jax.tree.unflatten(tree, refs)
    r = types.SimpleNamespace(**{name: ref for part in r for name, ref in part.items()})
    r.ringed = types.SimpleNamespace(**r.ringed)

    def load(number):
        src = (r.eo_hbm, r.hidden_hbm, r.wq_hbm, r.cot_hbm, r.wo_hbm, r.wk_hbm, r.wv_hbm)[number]
        w_pair = [r.wkv.at[:, pl.ds(at, 512)] for at in (0, 512)]
        dst = (r.eo, r.hidden, r.wq, r.cot, r.wo, *w_pair)[number]
        return pltpu.make_async_copy(src, dst, r.load_sems.at[number])

    def load_third(third):
        lanes = pl.ds(third * 1024, 1024)
        return pltpu.make_async_copy(r.qkv_hbm.at[:, lanes], r.qkv.at[:, lanes], r.load_sems.at[7 + third])

    for third in range(3):
        load_third(third).start()
    load(0).start()
    enc, gen, where, at = neighbours()
    x, y, z, core = where["x"], where["y"], where["z"], where["core"]
    barrier = pltpu.get_barrier_semaphore()
    loop(1, 16, lambda step: pl.semaphore_signal(barrier, inc=1, device_id=(enc, (gen + step) % 16), device_id_type=MESH))
    loop(1, 8, lambda step: pl.semaphore_signal(barrier, inc=1, device_id=((enc + step) % 8, gen), device_id_type=MESH))

    normalise(r.nbr, r.enc_gain, r.enc_normed)
    for third in range(3):
        load_third(third).wait()
        lanes = slice(third * 1024, third * 1024 + 1024)
        r.projected[:, lanes] = dot(r.enc_normed[...], r.qkv[:, lanes]).astype(jnp.bfloat16)
    for number in range(1, 7):
        load(number).start()
    loop(0, 2, lambda i: encoder_attention(i, r.projected, r.enc_normed))
    load(0).wait()
    for i in range(2):
        rows = slice(i * 128, i * 128 + 128)
        update = dot(r.enc_normed[rows, :], r.eo[...])
        r.encoded[i] = (r.nbr[rows, :].astype(jnp.float32) + update).astype(jnp.bfloat16)
    pl.semaphore_wait(barrier, 22)

    own_rows = rows_of(enc * 16, 16)

    def out_enc(half):
        lanes = pl.ds(half * 512, 512)

        def copy(step):
            peer = (enc + step) % 8
            return send(
                r.encoded.at[:, rows_of(peer * 16, 16), lanes],
                r.columns[half].at[pl.ds(enc * 2, 2)],
                r.s_oenc[half],
                step - 1,
                (peer, gen),
            )

        return Exchange(8, copy)

    def over_gen(half, target, sems):
        def copy(step):
            peer = (gen + step) % 16
            return send(
                r.outgoing[half].at[pl.ds(peer * 2, 2)],
                target[half].at[pl.ds(gen * 2, 2)],
                sems[half],
                step - 1,
                (enc, peer),
            )

        return Exchange(16, copy)

    out_encs = [out_enc(half) for half in range(HALVES)]
    out_gens = [over_gen(half, r.incoming, r.s_ogen) for half in range(HALVES)]
    for half in range(HALVES):
        out_encs[half].start()
    for half in range(HALVES):
        r.columns[half][pl.ds(enc * 2, 2)] = r.encoded[:, own_rows, half * 512 : half * 512 + 512]

    def start_out_gen(half):
        out_encs[half].receive()
        for j in range(32):
            r.outgoing[half][j] = r.columns[half][r.send[j]]
        out_gens[half].start()
        own = pl.ds(gen * 2, 2)
        r.incoming[half][own] = r.outgoing[half][own]

    def store_pairs(out, i, low):
        for block in range(4):
            for head in range(4):
                start = i * 1024 + block * 256 + head // 2 * 128 + head % 2 * 64
                out[rows_of(start, 64), head % 2 * 128 : head % 2 * 128 + 128] = low[
                    block * 64 : block * 64 + 64, head * 128 : head * 128 + 128
                ]

    def query_tile(i):
        low = dot(r.hidden[rows_of(i * 256, 256), :], r.wq[...]).astype(jnp.bfloat16)
        store_pairs(r.q_pairs, i, low)

    def cotangent_tile(i):
        low = dot(r.cot[rows_of(i * 256, 256), :], r.wo[...], ACROSS).astype(jnp.bfloat16)
        store_pairs(r.dm_pairs, i, low)

    r.q_pairs[...] = jnp.zeros_like(r.q_pairs)
    r.dm_pairs[...] = jnp.zeros_like(r.dm_pairs)
    load(1).wait()
    normalise(r.hidden, r.gain, r.hidden)
    load(2).wait()
    start_out_gen(0)
    loop(0, 1, query_tile)
    start_out_gen(1)
    loop(1, 2, query_tile)
    load(3).wait()
    load(4).wait()
    loop(0, 2, cotangent_tile)

    minus, plus, across = (z + 3) % 4 * 2 + core, (z + 1) % 4 * 2 + core, (z + 2) % 4 * 2 + core
    up, down, peer = at("z", 1), at("z", 3), at("core", 1)
    rings, crosses = [], []
    for half in range(HALVES):
        rows = r.rows.at[:, :, pl.ds(half * 512, 512)]
        first, second = pl.ds(0, 128), pl.ds(128, 128)

        def share(ref, sems, number, device):
            return send(ref, ref, sems, number, device)

        rings.append(
            [
                share(rows.at[enc], r.s_ring[half], 0, up),
                share(rows.at[enc], r.s_ring[half], 1, down),
                share(rows.at[minus, first], r.s_ring[half], 2, up),
                share(rows.at[plus, second], r.s_ring[half], 3, down),
            ]
        )
        crosses.append(
            [
                share(rows.at[enc], r.s_cross[half], 0, peer),
                share(rows.at[minus], r.s_cross[half], 1, peer),
                share(rows.at[plus], r.s_cross[half], 2, peer),
                share(rows.at[across, first], r.s_cross[half], 3, peer),
                share(rows.at[across, second], r.s_cross[half], 4, peer),
            ]
        )

    def take_slots(half):
        out_gens[half].receive()
        for j in range(16):
            r.rows[enc, j * 16 : j * 16 + 16, half * 512 : half * 512 + 512] = r.incoming[half][r.receive[j]]

    def gather_own(half):
        rings[half][0].start()
        rings[half][1].start()
        crosses[half][0].start()

    def gather_next(half):
        rings[half][0].wait_recv()
        rings[half][2].start()
        crosses[half][1].start()
        rings[half][1].wait_recv()
        rings[half][3].start()
        crosses[half][2].start()

    def gather_last(half):
        rings[half][2].wait_recv()
        crosses[half][3].start()
        rings[half][3].wait_recv()
        crosses[half][4].start()

    def of_peer(piece):
        return piece + 1 - 2 * core

    def project(piece):
        r.kv[piece] = dot(r.rows[piece], r.wkv[...]).astype(jnp.bfloat16)

    def project_some(pieces):
        def body(i):
            piece = pieces[0]
            for number in range(1, len(pieces)):
                piece = jnp.where(i == number, pieces[number], piece)
            project(piece)

        loop(0, len(pieces), body)

    load(5).wait()
    load(6).wait()
    take_slots(0)
    gather_own(0)
    take_slots(1)
    gather_next(0)
    gather_own(1)
    gather_last(0)
    crosses[1][0].wait_recv()
    crosses[0][0].wait_recv()
    project_some((enc, of_peer(enc)))
    gather_next(1)
    for number in (1, 2):
        crosses[0][number].wait_recv()
    project_some((minus, plus))
    for number in (1, 2):
        crosses[1][number].wait_recv()
    project_some((of_peer(minus), of_peer(plus)))
    gather_last(1)
    for number in (3, 4):
        crosses[0][number].wait_recv()
        crosses[1][number].wait_recv()
    project_some((across, of_peer(across)))

    ot_a, ot_b = r.wq.at[:, pl.ds(0, 256)], r.wq.at[:, pl.ds(256, 256)]
    kt, vt = r.eo.at[:, pl.ds(0, 512)], r.eo.at[:, pl.ds(512, 512)]
    mixed, mixed_t = r.hidden.at[:, pl.ds(0, 512)], r.hidden.at[:, pl.ds(512, 512)]
    ring_oa = Ring(ot_a, r.ringed.ota[0], r.ringed.ota[1], "x", where, at)
    ring_ob = Ring(ot_b, r.ringed.otb[0], r.ringed.otb[1], "y", where, at)
    ring_k = Ring(kt, r.ringed.kt[0], r.ringed.kt[1], "x", where, at)
    ring_v = Ring(vt, r.ringed.vt[0], r.ringed.vt[1], "y", where, at)
    ring_oa2 = Ring(r.ot_a2, r.ringed.ota2[0], r.ringed.ota2[1], "y", where, at)
    ring_ob2 = Ring(r.ot_b2, r.ringed.otb2[0], r.ringed.otb2[1], "x", where, at)
    ring_k2 = Ring(r.kt2, r.ringed.kt2[0], r.ringed.kt2[1], "y", where, at)
    ring_v2 = Ring(r.vt2, r.ringed.vt2[0], r.ringed.vt2[1], "x", where, at)
    mine = [r.qkv.at[:, pl.ds(half * 512, 512)] for half in range(HALVES)]
    peers = [r.qkv.at[:, pl.ds(1024 + half * 512, 512)] for half in range(HALVES)]
    from_peer = [r.qkv.at[:, pl.ds(2048 + half * 512, 512)] for half in range(HALVES)]
    ring_z = [Ring(mine[half], r.ring_z[half][0], r.ring_z[half][1], "z", where, at) for half in range(HALVES)]

    loop(0, 8, lambda b: attention_forward(b, r, mixed))
    mixed_t[...] = mixed[...].T

    def out_terms(i):
        to_x, to_y = (x + 2 - i + 4) % 4, (y + 2 - i + 4) % 4

        def tile(j):
            lane_a = pl.multiple_of((to_x * 4 + j) * 256, 256)
            term = dot(mixed_t[0:256, :], r.cot[:, pl.ds(lane_a, 256)])
            ot_a[pl.ds(lane_a, 256), :] = term.astype(jnp.bfloat16)
            lane_b = pl.multiple_of((j * 4 + to_y) * 256, 256)
            term = dot(mixed_t[256:512, :], r.cot[:, pl.ds(lane_b, 256)])
            ot_b[rows_of((to_y * 4 + j) * 256, 256), :] = term.astype(jnp.bfloat16)

        loop(0, 4, tile)

        @pl.when(i == 0)
        def _():
            ring_oa.first()
            ring_ob.first()

    loop(0, 4, out_terms)
    ring_oa.second()
    ring_ob.second()
    loop(0, 8, lambda b: attention_backward(b, r))
    ring_oa.third(64)
    ring_ob.third(64)

    core_copies = [
        [
            send(
                peers[half].at[pl.ds(k * 256, 256), :],
                from_peer[half].at[pl.ds(k * 256, 256), :],
                r.s_core[half],
                k,
                peer,
            )
            for k in range(4)
        ]
        for half in range(HALVES)
    ]

    def enc_piece(half, piece_at, out, out_at):
        feats = slice(half * 512, half * 512 + 512)
        term = dot(r.dkv[piece_at], r.wkv[feats, :], ACROSS)
        out[rows_of(out_at, 256), :] = term.astype(jnp.bfloat16)

    def enc_half(half):
        def to_peer(k):
            enc_piece(half, k * 2 + (1 - core), peers[half], k * 256)
            for number in range(4):

                @pl.when(k == number)
                def _():
                    core_copies[half][number].start()

        loop(0, 4, to_peer)
        loop(0, 4, lambda k: enc_piece(half, k * 2 + core, mine[half], k * 256))
        for k in range(4):
            core_copies[half][k].wait_recv()
        add_rows(mine[half], 0, ((mine[half], 0), (from_peer[half], 0)), 1024, 64)
        ring_z[half].first()
        ring_z[half].second()

    def key_terms(part):
        lanes = pl.ds(pl.multiple_of(part * 128, 128), 128)
        term = dot(r.rows[:, :, lanes].reshape(2048, 128), r.dkv[...].reshape(2048, 1024), DOWN)
        low = term.astype(jnp.bfloat16)
        kt[rows_of(part * 128, 128), :] = low[:, 0:512]
        for side in range(2):
            to_x, to_y = (part * 2 + side) // 4, (part * 2 + side) % 4
            vt[rows_of(to_y * 256 + to_x * 64, 64), :] = low[side * 64 : side * 64 + 64, 512:1024]

    enc_half(0)
    enc_half(1)
    loop(0, 4, key_terms)
    ring_z[0].third(64)
    loop(4, 8, key_terms)
    ring_k.first()
    ring_v.first()
    ring_k.second()
    ring_v.second()

    back_gens = [over_gen(half, r.returned, r.s_bgen) for half in range(HALVES)]

    def start_back_gen(half):
        ring_z[half].last(r.piece[half], 0, 16)
        out_gens[half].drain()
        for j in range(32):
            r.outgoing[half][j] = r.piece[half][r.position[j]]
        back_gens[half].start()
        own = pl.ds(gen * 2, 2)
        r.returned[half][own] = r.outgoing[half][own]

    def back_enc(half):
        def copy(step):
            to = (enc + step) % 8
            return send(
                r.grads[half].at[to],
                r.home.at[:, own_rows, pl.ds(half * 512, 512)],
                r.s_benc[half],
                step - 1,
                (to, gen),
            )

        return Exchange(8, copy)

    back_encs = [back_enc(half) for half in range(HALVES)]

    def start_back_enc(half):
        back_gens[half].receive()
        for j in range(16):
            r.grads[half][j // 2, j % 2] = r.returned[half][r.column[j]]
        back_encs[half].start()
        r.home[:, own_rows, half * 512 : half * 512 + 512] = r.grads[half][enc]

    start_back_gen(0)
    ring_z[1].third(64)
    ring_oa.last(r.ot_a2, 0, 64)
    ring_oa2.first()
    ring_oa2.second()
    ring_ob.last(r.ot_b2, 0, 64)
    ring_ob2.first()
    ring_ob2.second()
    ring_k.third(64)
    ring_v.third(64)
    ring_oa2.third(64)
    ring_ob2.third(64)
    start_back_gen(1)
    ring_k.last(r.kt2, 0, 64)
    ring_k2.first()
    ring_k2.second()
    ring_v.last(r.vt2, 0, 64)
    ring_v2.first()
    ring_v2.second()
    start_back_enc(0)
    ring_oa2.last(r.wo_out, 0, 64)
    ring_ob2.last(r.wo_out, 256, 64)
    ring_k2.third(32)
    ring_v2.third(32)
    start_back_enc(1)
    ring_k2.last(r.wk_out, 0, 32)
    ring_v2.last(r.wv_out, 0, 32)
    for half in range(HALVES):
        back_encs[half].receive()
    r.enc_out[...] = r.home[...]

    rings_all = [ring_oa, ring_ob, ring_k, ring_v, ring_oa2, ring_ob2, ring_k2, ring_v2] + ring_z
    for ring in rings_all:
        ring.drain()
    for half in range(HALVES):
        for copy in core_copies[half] + rings[half] + crosses[half]:
            copy.wait_send()
        for exchange in (out_encs[half], back_gens[half], back_encs[half]):
            exchange.drain()


def whole(tables, nbr, enc_gain, gain, qkv, eo, hidden, cot, wq, wo, wk, wv):
    low = jnp.bfloat16
    vmem = lambda *shape: pltpu.VMEM(shape, low)
    sems = lambda *shape: pltpu.SemaphoreType.DMA(shape)
    both = lambda make, *shape: [make(*shape) for _ in range(HALVES)]
    ring = lambda count, width: [vmem(count // 4 * 3, width), sems(2, 6)]
    anywhere = pl.BlockSpec(memory_space=pl.ANY)
    scalars = pl.BlockSpec(memory_space=pltpu.SMEM)
    local = pl.BlockSpec(memory_space=pltpu.VMEM)
    send_table, position_table, receive_table, column_table = tables
    small = dict(send=send_table, position=position_table, receive=receive_table, column=column_table)
    near = dict(nbr=nbr.reshape(256, 1024), enc_gain=enc_gain.reshape(1, -1), gain=gain.reshape(1, -1))
    big = dict(
        qkv_hbm=qkv, eo_hbm=eo, hidden_hbm=hidden, wq_hbm=wq, cot_hbm=cot, wo_hbm=wo, wk_hbm=wk, wv_hbm=wv
    )
    outputs = dict(
        enc_out=jax.ShapeDtypeStruct((2, 128, 1024), low),
        wo_out=jax.ShapeDtypeStruct((512, 256), low),
        wk_out=jax.ShapeDtypeStruct((64, 512), low),
        wv_out=jax.ShapeDtypeStruct((64, 512), low),
    )
    scratch = dict(
        qkv=vmem(1024, 3072),
        eo=vmem(1024, 1024),
        hidden=vmem(512, 4096),
        wq=vmem(4096, 512),
        cot=vmem(512, 4096),
        wo=vmem(512, 4096),
        wkv=vmem(1024, 1024),
        enc_normed=vmem(256, 1024),
        projected=vmem(256, 3072),
        encoded=vmem(2, 128, 1024),
        q_pairs=vmem(2048, 256),
        dm_pairs=vmem(2048, 256),
        kv=vmem(8, 256, 1024),
        dkv=vmem(8, 256, 1024),
        rows=vmem(8, 256, 1024),
        ot_a2=vmem(1024, 256),
        ot_b2=vmem(1024, 256),
        kt2=vmem(256, 512),
        vt2=vmem(256, 512),
        home=vmem(2, 128, 1024),
        ringed=dict(
            ota=ring(4096, 256),
            otb=ring(4096, 256),
            kt=ring(1024, 512),
            vt=ring(1024, 512),
            ota2=ring(1024, 256),
            otb2=ring(1024, 256),
            kt2=ring(256, 512),
            vt2=ring(256, 512),
        ),
        ring_z=both(ring, 1024, 512),
        columns=both(vmem, 16, 16, 512),
        outgoing=both(vmem, 32, 16, 512),
        incoming=both(vmem, 32, 16, 512),
        returned=both(vmem, 32, 16, 512),
        piece=both(vmem, 16, 16, 512),
        grads=both(vmem, 8, 2, 16, 512),
        s_oenc=both(sems, 2, 7),
        s_benc=both(sems, 2, 7),
        s_ogen=both(sems, 2, 15),
        s_bgen=both(sems, 2, 15),
        s_ring=both(sems, 2, 4),
        s_cross=both(sems, 2, 5),
        s_core=both(sems, 2, 4),
        load_sems=sems(10),
    )
    operands = small | near | big
    leaves, _ = jax.tree.flatten(scratch)
    tree = jax.tree.structure((operands, outputs, scratch))
    by_name = lambda part: [part[name] for name in sorted(part)]
    place = dict.fromkeys(small, scalars) | dict.fromkeys(near, local) | dict.fromkeys(big, anywhere)
    return pl.pallas_call(
        functools.partial(whole_kernel, tree),
        name="retro_whole",
        out_shape=tuple(by_name(outputs)),
        in_specs=by_name(place),
        out_specs=(local,) * len(outputs),
        scratch_shapes=leaves,
        compiler_params=pltpu.CompilerParams(
            collective_id=1, has_side_effects=True, vmem_limit_bytes=61 * 1024 * 1024
        ),
    )(*by_name(operands))


def widen_kernel(*refs):
    sources, targets, near, sems = refs[:4], refs[4:8], refs[8:12], refs[12]
    copies = [
        pltpu.make_async_copy(src, dst, sems.at[number]) for number, (src, dst) in enumerate(zip(sources, near))
    ]
    for copy in copies:
        copy.start()
    for copy, src, dst in zip(copies, near, targets):
        copy.wait()
        dst[...] = src[...].astype(jnp.float32)


def widen(values):
    return pl.pallas_call(
        widen_kernel,
        name="widen",
        out_shape=tuple(jax.ShapeDtypeStruct(value.shape, jnp.float32) for value in values),
        in_specs=[pl.BlockSpec(memory_space=pl.ANY)] * 4,
        out_specs=(pl.BlockSpec(memory_space=pltpu.VMEM),) * 4,
        scratch_shapes=[pltpu.VMEM(value.shape, value.dtype) for value in values] + [pltpu.SemaphoreType.DMA((4,))],
        compiler_params=pltpu.CompilerParams(vmem_limit_bytes=8 * 1024 * 1024),
    )(*values)


def routing(nbr_index, row_index, gen_count, per_device, row_size, capacity):
    entries = nbr_index.reshape(gen_count, row_size)
    source = entries // per_device % gen_count
    column = entries // (per_device * gen_count) * per_device + entries % per_device
    places = jnp.arange(row_size, dtype=jnp.int32)
    same = (source[:, :, None] == source[:, None, :]) & (places[None, None, :] < places[None, :, None])
    rank = jnp.sum(same.astype(jnp.int32), axis=2)
    rows = jnp.arange(gen_count, dtype=jnp.int32)
    send_slot = (rows[:, None] * capacity + rank).reshape(-1)
    mine = (source == row_index).reshape(-1)
    flat_column = column.reshape(-1)
    buffers = jnp.arange(gen_count * capacity, dtype=jnp.int32)
    send_match = (send_slot[:, None] == buffers[None, :]) & mine[:, None]
    send_column = jnp.sum(jnp.where(send_match, flat_column[:, None], 0), axis=0)
    column_match = (flat_column[:, None] == places[None, :]) & mine[:, None]
    column_position = jnp.sum(jnp.where(column_match, send_slot[:, None], 0), axis=0)
    own = (rows == row_index)[:, None]
    receive_position = jnp.sum(jnp.where(own, source * capacity + rank, 0), axis=0)
    receive_match = receive_position[:, None] == buffers[None, :]
    position_slot = jnp.sum(jnp.where(receive_match, places[:, None], 0), axis=0)
    return (send_column, position_slot, receive_position, column_position)


def local(
    hidden_states,
    grad_out,
    nbr_embed,
    nbr_index,
    gain,
    w_query,
    w_out,
    w_key,
    w_value,
    enc_gain,
    enc_qkv,
    enc_out,
):
    gen_count = lax.axis_size("gen")
    per_device = nbr_embed.shape[0]
    row_size = per_device * lax.axis_size("enc")
    capacity = max(2, 2 * row_size // gen_count)
    tables = routing(nbr_index, lax.axis_index("gen"), gen_count, per_device, row_size, capacity)
    grad_encoded, grad_key, grad_out_proj, grad_value = (
        whole(
            tables,
            nbr_embed,
            enc_gain,
            gain,
            enc_qkv,
            enc_out,
            hidden_states,
            grad_out,
            w_query,
            w_out,
            w_key,
            w_value,
        )
    )
    return widen((grad_encoded, grad_out_proj, grad_key, grad_value))


def solution(mesh):
    return jax.shard_map(
        local,
        mesh=mesh,
        in_specs=(
            P("gen", None),
            P("gen", None),
            P(("enc", "gen"), None, None),
            P(),
            P(),
            P(None, "enc"),
            P("enc", None),
            P(None, "enc"),
            P(None, "enc"),
            P(),
            P(),
            P(),
        ),
        out_specs=(
            P(("enc", "gen"), None, None),
            P("enc", "gen"),
            P("gen", "enc"),
            P("gen", "enc"),
        ),
        check_vma=False,
    )
```

time: 664 us -> 141 us (0.21); the launches traced: 655 us -> 141 us
  waiting for transfers between devices: 456 us -> 0 us
  Pallas kernels: 0 us -> 133 us
  matrix products: 82 us -> 0 us
  local copies, waits for them, and re-layouts: 48.9 us -> 4.75 us
  other arithmetic: 36.3 us -> 2.44 us
  starting transfers between devices: 17.4 us -> 0 us
  between operations: 14.4 us -> 0.87 us
    all_to_all x2 -> x0, waiting for transfers between devices: 262 us -> none  [the longest x1 132 us: local(): lax.all_to_all(outgoing, 'gen', split_axis=0, concat_axis=0, tiled=True)]
    reduce_scatter x4 -> x0, waiting for transfers between devices: 160 us -> none  [the longest x1 79.4 us: local(): lax.psum_scatter(out_term.astype(jnp.bfloat16), 'gen', scatter_dimension=...]
    pallas_call x0 -> x2, Pallas kernels: none -> 133 us  [the longest x1 132 us: whole(): pl.pallas_call(functools.partial(whole_kernel, tree), name='retro_whole',...]
    dot_general x18 -> x0, matrix products: 82 us -> none  [the longest x1 16 us: attention_grads(): jnp.einsum('bhqk,bqhd->bkhd', d_raw, queries, preferred_element_type=jnp....]
    all_gather x1 -> x0, waiting for transfers between devices: 34.8 us -> none  [local(): row_encoded = lax.all_gather(encoded, 'enc', axis=0, tiled=True)]
    gather x4 -> x0, local copies, waits for them, and re-layouts: 26.6 us -> none  [the longest x1 7.16 us: local(): returning = jnp.take(enc_term_low, position_slot, axis=0)]
    select_n x8 -> x1, other arithmetic: 22.4 us -> 0.02 us  [routing(): source = entries // per_device % gen_count]
    all_to_all x2 -> x0, starting transfers between devices: 16.6 us -> none  [the longest x1 9.84 us: local(): lax.all_to_all(returning, 'gen', split_axis=0, concat_axis=0, tiled=True)]
  transfers between devices with their start and end apart: 7 -> 0, of which waited for: 6 -> 0; matrix products, arithmetic and copies ran while one was open for 12% -> 0% of each run, Pallas kernels for 0% -> 0%
where the time goes in v4:
time: 141 us
  Pallas kernels  133 us (94%)
  local copies, waits for them, and re-layouts  4.75 us (3%)
  other arithmetic  2.44 us (2%)
    pallas_call x1, Pallas kernels, whole(): pl.pallas_call(functools.partial(whole_kernel, tree), name='retro_whole',...  132 us
    unnamed x11, local copies, waits for them, and re-layouts  4.45 us

profile of v4, /device:TPU:1, one launch (start us, length us, event | category | flops | bytes accessed | tf_op | source)
XLA Modules:
  0.0 141.2 jit_solution(9903929821036571165)
XLA Ops:
  0.7 0.8 copy.18
  1.5 0.1 reshape.218
  1.6 0.1 reshape.219
  1.7 0.4 convert_reduce_fusion
  2.2 0.1 select_reduce_fusion.3
  2.3 0.0 copy-start.4
  2.3 0.1 add.77
  2.4 0.6 select_reduce_fusion.refs_10_
  3.0 0.6 select_reduce_fusion.1.refs_0_
  3.6 0.6 select_reduce_fusion.2.refs_7_
  4.2 0.0 copy-done.4
  4.2 131.5 %retro_whole.1 = (bf16[2,128,1024]{2,1,0:T(8,128)(2,1)}, bf16[64,512]{1,0:T(8,128)(2,1)}, bf16[512,256]{1,0:T(8,128)(2,1)}, bf16[64,512]{1,0:T(8,128)(2,1)}) custom-call(s32[16]{0:T(128)} %select_reduce_fusion.1.refs_0_, bf16[512,4096]{1,0:T(8,128)(2,1)} %refs_1_.1, f32[1,1024]{1,0:T(1,128)} %bitcast.5, bf16[1024,1024]{1,0:T(8,128)(2,1)} %refs_3_.1, ...), custom_call_target="tpu_custom_call" | custom-call | tf_op jit(solution)/shard_map/retro_whole/pallas_call | solution.py:671
  135.8 0.0 copy-start
  135.8 1.0 copy-done
  136.8 0.0 copy-start.1
  136.8 0.9 copy-done.1
  137.7 0.0 copy-start.2
  137.7 0.8 copy-done.2
  138.6 0.0 copy-start.3
  138.6 0.8 copy-done.3
  139.4 1.6 %widen.1 = (f32[2,128,1024]{2,1,0:T(8,128)}, f32[512,256]{1,0:T(8,128)}, f32[64,512]{1,0:T(8,128)}, f32[64,512]{1,0:T(8,128)}) custom-call(bf16[2,128,1024]{2,1,0:T(8,128)(2,1)S(1)} %copy-done, bf16[512,256]{1,0:T(8,128)(2,1)S(1)} %copy-done.1, bf16[64,512]{1,0:T(8,128)(2,1)S(1)} %copy-done.2, bf16[64,512]{1,0:T(8,128)(2,1)S(1)} %copy-done.3), custom_call_target="tpu_custom_call" | custom-call | tf_op jit(solution)/shard_map/widen/pallas_call | solution.py:697
  (6 shorter events, 0.1 us)
Async XLA Ops:
  2.3 2.0 %copy-start.4 = (s32[16]{0:T(128)}, s32[16]{0:T(128)S(1)}, u32[]{:S(2)}) copy-start(s32[16]{0:T(128)S(1)} %get-tuple-element.12.refs_9_) | copy-start | bytes 196
  135.8 1.0 copy-start
  136.8 0.9 copy-start.1
  137.7 0.8 copy-start.2
  138.6 0.8 copy-start.3

commit v5 on v4

--- a/solution.py
+++ b/solution.py
@@ -95,13 +95,17 @@
         self.copies[1].start()
         self.copies[4].start()
 
-    def third(self, step):
+    def third(self, step, with_second=False):
         half = self.half
         self.copies[0].wait_recv()
+        if with_second:
+            self.copies[3].wait_recv()
+            self.second()
         start = self.plus * self.rows
         add_rows(self.src, start, ((self.src, start), (self.buf, 0)), half, step)
         self.copies[2].start()
-        self.copies[3].wait_recv()
+        if not with_second:
+            self.copies[3].wait_recv()
         start = self.minus * self.rows + half
         add_rows(self.src, start, ((self.src, start), (self.buf, 3 * half)), half, step)
         self.copies[5].start()
@@ -251,10 +255,14 @@
         load(number).start()
     loop(0, 2, lambda i: encoder_attention(i, r.projected, r.enc_normed))
     load(0).wait()
-    for i in range(2):
-        rows = slice(i * 128, i * 128 + 128)
-        update = dot(r.enc_normed[rows, :], r.eo[...])
-        r.encoded[i] = (r.nbr[rows, :].astype(jnp.float32) + update).astype(jnp.bfloat16)
+
+    def finish(half):
+        lanes = slice(half * 512, half * 512 + 512)
+        update = dot(r.enc_normed[...], r.eo[:, lanes])
+        low = (r.nbr[:, lanes].astype(jnp.float32) + update).astype(jnp.bfloat16)
+        r.encoded[:, :, lanes] = low.reshape(2, 128, 512)
+
+    finish(0)
     pl.semaphore_wait(barrier, 22)
 
     own_rows = rows_of(enc * 16, 16)
@@ -289,16 +297,14 @@
 
     out_encs = [out_enc(half) for half in range(HALVES)]
     out_gens = [over_gen(half, r.incoming, r.s_ogen) for half in range(HALVES)]
-    for half in range(HALVES):
-        out_encs[half].start()
+    out_encs[0].start()
+    finish(1)
     for half in range(HALVES):
         r.columns[half][pl.ds(enc * 2, 2)] = r.encoded[:, own_rows, half * 512 : half * 512 + 512]
 
-    def start_out_gen(half):
-        out_encs[half].receive()
+    def pick_out_gen(half):
         for j in range(32):
             r.outgoing[half][j] = r.columns[half][r.send[j]]
-        out_gens[half].start()
         own = pl.ds(gen * 2, 2)
         r.incoming[half][own] = r.outgoing[half][own]
 
@@ -320,16 +326,18 @@
 
     r.q_pairs[...] = jnp.zeros_like(r.q_pairs)
     r.dm_pairs[...] = jnp.zeros_like(r.dm_pairs)
+    out_encs[0].receive()
+    out_encs[1].start()
+    pick_out_gen(0)
+    out_gens[0].start()
     load(1).wait()
     normalise(r.hidden, r.gain, r.hidden)
     load(2).wait()
-    start_out_gen(0)
-    loop(0, 1, query_tile)
-    start_out_gen(1)
-    loop(1, 2, query_tile)
+    loop(0, 2, query_tile)
+    out_encs[1].receive()
+    pick_out_gen(1)
     load(3).wait()
     load(4).wait()
-    loop(0, 2, cotangent_tile)
 
     minus, plus, across = (z + 3) % 4 * 2 + core, (z + 1) % 4 * 2 + core, (z + 2) % 4 * 2 + core
     up, down, peer = at("z", 1), at("z", 3), at("core", 1)
@@ -401,11 +409,13 @@
     load(5).wait()
     load(6).wait()
     take_slots(0)
+    out_gens[1].start()
     gather_own(0)
+    loop(0, 2, cotangent_tile)
+    gather_next(0)
+    gather_last(0)
     take_slots(1)
-    gather_next(0)
     gather_own(1)
-    gather_last(0)
     crosses[1][0].wait_recv()
     crosses[0][0].wait_recv()
     project_some((enc, of_peer(enc)))
@@ -463,8 +473,6 @@
     ring_oa.second()
     ring_ob.second()
     loop(0, 8, lambda b: attention_backward(b, r))
-    ring_oa.third(64)
-    ring_ob.third(64)
 
     core_copies = [
         [
@@ -496,11 +504,11 @@
 
         loop(0, 4, to_peer)
         loop(0, 4, lambda k: enc_piece(half, k * 2 + core, mine[half], k * 256))
+
+    def add_peer(half):
         for k in range(4):
             core_copies[half][k].wait_recv()
         add_rows(mine[half], 0, ((mine[half], 0), (from_peer[half], 0)), 1024, 64)
-        ring_z[half].first()
-        ring_z[half].second()
 
     def key_terms(part):
         lanes = pl.ds(pl.multiple_of(part * 128, 128), 128)
@@ -512,10 +520,15 @@
             vt[rows_of(to_y * 256 + to_x * 64, 64), :] = low[side * 64 : side * 64 + 64, 512:1024]
 
     enc_half(0)
+    add_peer(0)
+    ring_z[0].first()
+    ring_oa.third(64)
+    ring_ob.third(64)
     enc_half(1)
-    loop(0, 4, key_terms)
-    ring_z[0].third(64)
-    loop(4, 8, key_terms)
+    ring_z[0].third(64, True)
+    add_peer(1)
+    loop(0, 8, key_terms)
+    ring_z[1].first()
     ring_k.first()
     ring_v.first()
     ring_k.second()
@@ -555,7 +568,7 @@
         r.home[:, own_rows, half * 512 : half * 512 + 512] = r.grads[half][enc]
 
     start_back_gen(0)
-    ring_z[1].third(64)
+    ring_z[1].third(64, True)
     ring_oa.last(r.ot_a2, 0, 64)
     ring_oa2.first()
     ring_oa2.second()
@@ -701,7 +714,7 @@
         in_specs=[pl.BlockSpec(memory_space=pl.ANY)] * 4,
         out_specs=(pl.BlockSpec(memory_space=pltpu.VMEM),) * 4,
         scratch_shapes=[pltpu.VMEM(value.shape, value.dtype) for value in values] + [pltpu.SemaphoreType.DMA((4,))],
-        compiler_params=pltpu.CompilerParams(vmem_limit_bytes=8 * 1024 * 1024),
+        compiler_params=pltpu.CompilerParams(vmem_limit_bytes=60 * 1024 * 1024),
     )(*values)
 
 

time: 141 us -> 135 us (0.957)
  local copies, waits for them, and re-layouts: 4.75 us -> 1.09 us
  Pallas kernels: 133 us -> 130 us
    unnamed x11 -> x3, local copies, waits for them, and re-layouts: 4.45 us -> 0.79 us
    pallas_call x1, Pallas kernels: 132 us -> 128 us  [whole(): pl.pallas_call(functools.partial(whole_kernel, tree), name='retro_whole',...]
where the time goes in v5:
time: 135 us
  Pallas kernels  130 us (96%)
  other arithmetic  2.44 us (2%)
    pallas_call x1, Pallas kernels, whole(): pl.pallas_call(functools.partial(whole_kernel, tree), name='retro_whole',...  128 us

profile of v5, /device:TPU:1, one launch (start us, length us, event | category | flops | bytes accessed | tf_op | source)
XLA Modules:
  0.0 134.6 jit_solution(15076574981074771395)
XLA Ops:
  0.7 0.8 copy.18
  1.5 0.1 reshape.218
  1.6 0.1 reshape.219
  1.7 0.4 convert_reduce_fusion
  2.2 0.1 select_reduce_fusion.3
  2.3 0.0 copy-start
  2.3 0.1 add.77
  2.4 0.6 select_reduce_fusion.refs_10_
  3.0 0.6 select_reduce_fusion.1.refs_0_
  3.6 0.6 select_reduce_fusion.2.refs_7_
  4.2 0.0 copy-done
  4.2 127.9 %retro_whole.1 = (bf16[2,128,1024]{2,1,0:T(8,128)(2,1)}, bf16[64,512]{1,0:T(8,128)(2,1)}, bf16[512,256]{1,0:T(8,128)(2,1)}, bf16[64,512]{1,0:T(8,128)(2,1)}) custom-call(s32[16]{0:T(128)} %select_reduce_fusion.1.refs_0_, bf16[512,4096]{1,0:T(8,128)(2,1)} %refs_1_.1, f32[1,1024]{1,0:T(1,128)} %bitcast.5, bf16[1024,1024]{1,0:T(8,128)(2,1)} %refs_3_.1, ...), custom_call_target="tpu_custom_call" | custom-call | tf_op jit(solution)/shard_map/retro_whole/pallas_call | solution.py:684
  132.2 2.4 %widen.1 = (f32[2,128,1024]{2,1,0:T(8,128)}, f32[512,256]{1,0:T(8,128)}, f32[64,512]{1,0:T(8,128)}, f32[64,512]{1,0:T(8,128)}) custom-call(bf16[2,128,1024]{2,1,0:T(8,128)(2,1)} %get-tuple-element.8.refs_0_, bf16[512,256]{1,0:T(8,128)(2,1)} %get-tuple-element.9.refs_1_, bf16[64,512]{1,0:T(8,128)(2,1)} %get-tuple-element.10.refs_2_, ...), custom_call_target="tpu_custom_call" | custom-call | tf_op jit(solution)/shard_map/widen/pallas_call | solution.py:710
  (6 shorter events, 0.1 us)
Async XLA Ops:
  2.3 2.0 %copy-start = (s32[16]{0:T(128)}, s32[16]{0:T(128)S(1)}, u32[]{:S(2)}) copy-start(s32[16]{0:T(128)S(1)} %get-tuple-element.12.refs_9_) | copy-start | bytes 196

commit v6 on v5

--- a/solution.py
+++ b/solution.py
@@ -188,8 +188,12 @@
     tokens = rows_of(b * CH, CH)
     for p in range(2):
         keys, rows, k, v = pair_refs(b, p, r)
-        _, probs = pair_probs(k, r.q_pairs[rows, :])
-        both = dot(probs.astype(jnp.bfloat16), v, DOWN).astype(jnp.bfloat16)
+        slope, probs = pair_probs(k, r.q_pairs[rows, :])
+        low = probs.astype(jnp.bfloat16)
+        lanes = pl.ds(pl.multiple_of((b * 2 + p) * 128, 128), 128)
+        r.wo[0:256, lanes] = low
+        r.wo[256:512, lanes] = ((1.0 - slope * slope) * 128 ** (-0.5)).astype(jnp.bfloat16)
+        both = dot(low, v, DOWN).astype(jnp.bfloat16)
         mixed[tokens, p * 256 : p * 256 + 128] = both[0:64, 0:128]
         mixed[tokens, p * 256 + 128 : p * 256 + 256] = both[64:128, 128:256]
 
@@ -198,12 +202,14 @@
     for p in range(2):
         keys, rows, k, v = pair_refs(b, p, r)
         q_pair, dm_pair = r.q_pairs[rows, :], r.dm_pairs[rows, :]
-        slope, probs = pair_probs(k, q_pair)
+        lanes = pl.ds(pl.multiple_of((b * 2 + p) * 128, 128), 128)
+        low, slope = r.wo[0:256, lanes], r.wo[256:512, lanes].astype(jnp.float32)
+        probs = low.astype(jnp.float32)
         d_probs = dot(v, dm_pair, ACROSS)
         d_capped = probs * (d_probs - jnp.sum(probs * d_probs, axis=0, keepdims=True))
-        d_raw = (d_capped * (1.0 - slope * slope) * 128 ** (-0.5)).astype(jnp.bfloat16)
+        d_raw = (d_capped * slope).astype(jnp.bfloat16)
         d_keys = dot(d_raw, q_pair).astype(jnp.bfloat16)
-        d_values = dot(probs.astype(jnp.bfloat16), dm_pair).astype(jnp.bfloat16)
+        d_values = dot(low, dm_pair).astype(jnp.bfloat16)
         r.dkv[:, keys, p * 256 : p * 256 + 256] = d_keys.reshape(8, 32, 256)
         r.dkv[:, keys, 512 + p * 256 : 512 + p * 256 + 256] = d_values.reshape(8, 32, 256)
 
@@ -464,14 +470,9 @@
 
         loop(0, 4, tile)
 
-        @pl.when(i == 0)
-        def _():
-            ring_oa.first()
-            ring_ob.first()
-
-    loop(0, 4, out_terms)
-    ring_oa.second()
-    ring_ob.second()
+    loop(0, 1, out_terms)
+    ring_oa.first()
+    ring_ob.first()
     loop(0, 8, lambda b: attention_backward(b, r))
 
     core_copies = [
@@ -522,17 +523,16 @@
     enc_half(0)
     add_peer(0)
     ring_z[0].first()
+    loop(1, 4, out_terms)
+    ring_oa.second()
+    ring_ob.second()
     ring_oa.third(64)
     ring_ob.third(64)
+    ring_z[0].third(64, True)
     enc_half(1)
-    ring_z[0].third(64, True)
     add_peer(1)
-    loop(0, 8, key_terms)
     ring_z[1].first()
-    ring_k.first()
-    ring_v.first()
-    ring_k.second()
-    ring_v.second()
+    loop(0, 4, key_terms)
 
     back_gens = [over_gen(half, r.returned, r.s_bgen) for half in range(HALVES)]
 
@@ -569,24 +569,29 @@
 
     start_back_gen(0)
     ring_z[1].third(64, True)
+    loop(4, 8, key_terms)
+    ring_k.first()
+    ring_v.first()
+    ring_k.second()
+    ring_v.second()
     ring_oa.last(r.ot_a2, 0, 64)
     ring_oa2.first()
     ring_oa2.second()
     ring_ob.last(r.ot_b2, 0, 64)
     ring_ob2.first()
     ring_ob2.second()
+    start_back_gen(1)
     ring_k.third(64)
     ring_v.third(64)
     ring_oa2.third(64)
     ring_ob2.third(64)
-    start_back_gen(1)
+    start_back_enc(0)
     ring_k.last(r.kt2, 0, 64)
     ring_k2.first()
     ring_k2.second()
     ring_v.last(r.vt2, 0, 64)
     ring_v2.first()
     ring_v2.second()
-    start_back_enc(0)
     ring_oa2.last(r.wo_out, 0, 64)
     ring_ob2.last(r.wo_out, 256, 64)
     ring_k2.third(32)

time: 135 us -> 132 us (0.978)
  Pallas kernels: 130 us -> 128 us
    pallas_call x1, Pallas kernels: 128 us -> 126 us  [whole(): pl.pallas_call(functools.partial(whole_kernel, tree), name='retro_whole',...]
where the time goes in v6:
time: 132 us
  Pallas kernels  128 us (97%)
  other arithmetic  2.44 us (2%)
    pallas_call x1, Pallas kernels, whole(): pl.pallas_call(functools.partial(whole_kernel, tree), name='retro_whole',...  126 us

profile of v6, /device:TPU:1, one launch (start us, length us, event | category | flops | bytes accessed | tf_op | source)
XLA Modules:
  0.0 132.2 jit_solution(13984968750290128775)
XLA Ops:
  0.7 0.8 copy.18
  1.5 0.1 reshape.218
  1.6 0.1 reshape.219
  1.7 0.4 convert_reduce_fusion
  2.2 0.1 select_reduce_fusion.3
  2.3 0.0 copy-start
  2.3 0.1 add.77
  2.4 0.6 select_reduce_fusion.refs_10_
  3.0 0.6 select_reduce_fusion.1.refs_0_
  3.6 0.6 select_reduce_fusion.2.refs_7_
  4.2 0.0 copy-done
  4.2 125.5 %retro_whole.1 = (bf16[2,128,1024]{2,1,0:T(8,128)(2,1)}, bf16[64,512]{1,0:T(8,128)(2,1)}, bf16[512,256]{1,0:T(8,128)(2,1)}, bf16[64,512]{1,0:T(8,128)(2,1)}) custom-call(s32[16]{0:T(128)} %select_reduce_fusion.1.refs_0_, bf16[512,4096]{1,0:T(8,128)(2,1)} %refs_1_.1, f32[1,1024]{1,0:T(1,128)} %bitcast.5, bf16[1024,1024]{1,0:T(8,128)(2,1)} %refs_3_.1, ...), custom_call_target="tpu_custom_call" | custom-call | tf_op jit(solution)/shard_map/retro_whole/pallas_call | solution.py:689
  129.8 2.4 %widen.1 = (f32[2,128,1024]{2,1,0:T(8,128)}, f32[512,256]{1,0:T(8,128)}, f32[64,512]{1,0:T(8,128)}, f32[64,512]{1,0:T(8,128)}) custom-call(bf16[2,128,1024]{2,1,0:T(8,128)(2,1)} %get-tuple-element.8.refs_0_, bf16[512,256]{1,0:T(8,128)(2,1)} %get-tuple-element.9.refs_1_, bf16[64,512]{1,0:T(8,128)(2,1)} %get-tuple-element.10.refs_2_, ...), custom_call_target="tpu_custom_call" | custom-call | tf_op jit(solution)/shard_map/widen/pallas_call | solution.py:715
  (6 shorter events, 0.1 us)
Async XLA Ops:
  2.3 2.0 %copy-start = (s32[16]{0:T(128)}, s32[16]{0:T(128)S(1)}, u32[]{:S(2)}) copy-start(s32[16]{0:T(128)S(1)} %get-tuple-element.12.refs_9_) | copy-start | bytes 196

commit v7 on v6

--- a/solution.py
+++ b/solution.py
@@ -419,9 +419,9 @@
     gather_own(0)
     loop(0, 2, cotangent_tile)
     gather_next(0)
-    gather_last(0)
     take_slots(1)
     gather_own(1)
+    gather_last(0)
     crosses[1][0].wait_recv()
     crosses[0][0].wait_recv()
     project_some((enc, of_peer(enc)))
@@ -473,6 +473,9 @@
     loop(0, 1, out_terms)
     ring_oa.first()
     ring_ob.first()
+    loop(1, 4, out_terms)
+    ring_oa.second()
+    ring_ob.second()
     loop(0, 8, lambda b: attention_backward(b, r))
 
     core_copies = [
@@ -523,16 +526,18 @@
     enc_half(0)
     add_peer(0)
     ring_z[0].first()
-    loop(1, 4, out_terms)
-    ring_oa.second()
-    ring_ob.second()
     ring_oa.third(64)
     ring_ob.third(64)
+    loop(0, 4, key_terms)
     ring_z[0].third(64, True)
+    loop(4, 8, key_terms)
+    ring_k.first()
+    ring_v.first()
+    ring_k.second()
+    ring_v.second()
     enc_half(1)
     add_peer(1)
     ring_z[1].first()
-    loop(0, 4, key_terms)
 
     back_gens = [over_gen(half, r.returned, r.s_bgen) for half in range(HALVES)]
 
@@ -568,23 +573,18 @@
         r.home[:, own_rows, half * 512 : half * 512 + 512] = r.grads[half][enc]
 
     start_back_gen(0)
-    ring_z[1].third(64, True)
-    loop(4, 8, key_terms)
-    ring_k.first()
-    ring_v.first()
-    ring_k.second()
-    ring_v.second()
     ring_oa.last(r.ot_a2, 0, 64)
     ring_oa2.first()
     ring_oa2.second()
     ring_ob.last(r.ot_b2, 0, 64)
     ring_ob2.first()
     ring_ob2.second()
-    start_back_gen(1)
+    ring_z[1].third(64, True)
     ring_k.third(64)
     ring_v.third(64)
     ring_oa2.third(64)
     ring_ob2.third(64)
+    start_back_gen(1)
     start_back_enc(0)
     ring_k.last(r.kt2, 0, 64)
     ring_k2.first()

time: 132 us -> 126 us (0.955)
  Pallas kernels: 128 us -> 122 us
    pallas_call x1, Pallas kernels: 126 us -> 120 us  [whole(): pl.pallas_call(functools.partial(whole_kernel, tree), name='retro_whole',...]
where the time goes in v7:
time: 126 us
  Pallas kernels  122 us (97%)
  other arithmetic  2.44 us (2%)
    pallas_call x1, Pallas kernels, whole(): pl.pallas_call(functools.partial(whole_kernel, tree), name='retro_whole',...  120 us

profile of v7, /device:TPU:1, one launch (start us, length us, event | category | flops | bytes accessed | tf_op | source)
XLA Modules:
  0.0 126.3 jit_solution(17105629211641116173)
XLA Ops:
  0.7 0.8 copy.18
  1.5 0.1 reshape.218
  1.6 0.1 reshape.219
  1.7 0.4 convert_reduce_fusion
  2.2 0.1 select_reduce_fusion.3
  2.3 0.0 copy-start
  2.3 0.1 add.77
  2.4 0.6 select_reduce_fusion.refs_10_
  3.0 0.6 select_reduce_fusion.1.refs_0_
  3.6 0.6 select_reduce_fusion.2.refs_7_
  4.2 0.0 copy-done
  4.2 119.6 %retro_whole.1 = (bf16[2,128,1024]{2,1,0:T(8,128)(2,1)}, bf16[64,512]{1,0:T(8,128)(2,1)}, bf16[512,256]{1,0:T(8,128)(2,1)}, bf16[64,512]{1,0:T(8,128)(2,1)}) custom-call(s32[16]{0:T(128)} %select_reduce_fusion.1.refs_0_, bf16[512,4096]{1,0:T(8,128)(2,1)} %refs_1_.1, f32[1,1024]{1,0:T(1,128)} %bitcast.5, bf16[1024,1024]{1,0:T(8,128)(2,1)} %refs_3_.1, ...), custom_call_target="tpu_custom_call" | custom-call | tf_op jit(solution)/shard_map/retro_whole/pallas_call | solution.py:689
  123.9 2.4 %widen.1 = (f32[2,128,1024]{2,1,0:T(8,128)}, f32[512,256]{1,0:T(8,128)}, f32[64,512]{1,0:T(8,128)}, f32[64,512]{1,0:T(8,128)}) custom-call(bf16[2,128,1024]{2,1,0:T(8,128)(2,1)} %get-tuple-element.8.refs_0_, bf16[512,256]{1,0:T(8,128)(2,1)} %get-tuple-element.9.refs_1_, bf16[64,512]{1,0:T(8,128)(2,1)} %get-tuple-element.10.refs_2_, ...), custom_call_target="tpu_custom_call" | custom-call | tf_op jit(solution)/shard_map/widen/pallas_call | solution.py:715
  (6 shorter events, 0.1 us)
Async XLA Ops:
  2.3 2.0 %copy-start = (s32[16]{0:T(128)}, s32[16]{0:T(128)S(1)}, u32[]{:S(2)}) copy-start(s32[16]{0:T(128)S(1)} %get-tuple-element.12.refs_9_) | copy-start | bytes 196

commit v8 on v7

--- a/solution.py
+++ b/solution.py
@@ -357,10 +357,12 @@
 
         rings.append(
             [
-                share(rows.at[enc], r.s_ring[half], 0, up),
-                share(rows.at[enc], r.s_ring[half], 1, down),
+                share(rows.at[enc, first], r.s_ring[half], 0, up),
+                share(rows.at[enc, second], r.s_ring[half], 1, down),
                 share(rows.at[minus, first], r.s_ring[half], 2, up),
                 share(rows.at[plus, second], r.s_ring[half], 3, down),
+                share(rows.at[enc, second], r.s_ring[half], 4, up),
+                share(rows.at[enc, first], r.s_ring[half], 5, down),
             ]
         )
         crosses.append(
@@ -381,14 +383,18 @@
     def gather_own(half):
         rings[half][0].start()
         rings[half][1].start()
+        rings[half][4].start()
+        rings[half][5].start()
         crosses[half][0].start()
 
     def gather_next(half):
         rings[half][0].wait_recv()
         rings[half][2].start()
-        crosses[half][1].start()
         rings[half][1].wait_recv()
         rings[half][3].start()
+        rings[half][4].wait_recv()
+        crosses[half][1].start()
+        rings[half][5].wait_recv()
         crosses[half][2].start()
 
     def gather_last(half):
@@ -415,8 +421,8 @@
     load(5).wait()
     load(6).wait()
     take_slots(0)
+    gather_own(0)
     out_gens[1].start()
-    gather_own(0)
     loop(0, 2, cotangent_tile)
     gather_next(0)
     take_slots(1)
@@ -433,10 +439,11 @@
         crosses[1][number].wait_recv()
     project_some((of_peer(minus), of_peer(plus)))
     gather_last(1)
+    project_some((across,))
     for number in (3, 4):
         crosses[0][number].wait_recv()
         crosses[1][number].wait_recv()
-    project_some((across, of_peer(across)))
+    project_some((of_peer(across),))
 
     ot_a, ot_b = r.wq.at[:, pl.ds(0, 256)], r.wq.at[:, pl.ds(256, 256)]
     kt, vt = r.eo.at[:, pl.ds(0, 512)], r.eo.at[:, pl.ds(512, 512)]
@@ -676,7 +683,7 @@
         s_benc=both(sems, 2, 7),
         s_ogen=both(sems, 2, 15),
         s_bgen=both(sems, 2, 15),
-        s_ring=both(sems, 2, 4),
+        s_ring=both(sems, 2, 6),
         s_cross=both(sems, 2, 5),
         s_core=both(sems, 2, 4),
         load_sems=sems(10),

time: 126 us -> 125 us (level)
    pallas_call x1, Pallas kernels: 120 us -> 118 us  [whole(): pl.pallas_call(functools.partial(whole_kernel, tree), name='retro_whole',...]
where the time goes in v8:
time: 125 us
  Pallas kernels  121 us (97%)
  other arithmetic  2.44 us (2%)
    pallas_call x1, Pallas kernels, whole(): pl.pallas_call(functools.partial(whole_kernel, tree), name='retro_whole',...  118 us

profile of v8, /device:TPU:1, one launch (start us, length us, event | category | flops | bytes accessed | tf_op | source)
XLA Modules:
  0.0 124.8 jit_solution(11550434079016662312)
XLA Ops:
  0.7 0.8 copy.18
  1.5 0.1 reshape.218
  1.6 0.1 reshape.219
  1.7 0.4 convert_reduce_fusion
  2.2 0.1 select_reduce_fusion.3
  2.3 0.0 copy-start
  2.3 0.1 add.77
  2.4 0.6 select_reduce_fusion.refs_10_
  3.0 0.6 select_reduce_fusion.1.refs_0_
  3.6 0.6 select_reduce_fusion.2.refs_7_
  4.2 0.0 copy-done
  4.2 118.2 %retro_whole.1 = (bf16[2,128,1024]{2,1,0:T(8,128)(2,1)}, bf16[64,512]{1,0:T(8,128)(2,1)}, bf16[512,256]{1,0:T(8,128)(2,1)}, bf16[64,512]{1,0:T(8,128)(2,1)}) custom-call(s32[16]{0:T(128)} %select_reduce_fusion.1.refs_0_, bf16[512,4096]{1,0:T(8,128)(2,1)} %refs_1_.1, f32[1,1024]{1,0:T(1,128)} %bitcast.5, bf16[1024,1024]{1,0:T(8,128)(2,1)} %refs_3_.1, ...), custom_call_target="tpu_custom_call" | custom-call | tf_op jit(solution)/shard_map/retro_whole/pallas_call | solution.py:696
  122.4 2.4 %widen.1 = (f32[2,128,1024]{2,1,0:T(8,128)}, f32[512,256]{1,0:T(8,128)}, f32[64,512]{1,0:T(8,128)}, f32[64,512]{1,0:T(8,128)}) custom-call(bf16[2,128,1024]{2,1,0:T(8,128)(2,1)} %get-tuple-element.8.refs_0_, bf16[512,256]{1,0:T(8,128)(2,1)} %get-tuple-element.9.refs_1_, bf16[64,512]{1,0:T(8,128)(2,1)} %get-tuple-element.10.refs_2_, ...), custom_call_target="tpu_custom_call" | custom-call | tf_op jit(solution)/shard_map/widen/pallas_call | solution.py:722
  (6 shorter events, 0.1 us)
Async XLA Ops:
  2.3 2.0 %copy-start = (s32[16]{0:T(128)}, s32[16]{0:T(128)S(1)}, u32[]{:S(2)}) copy-start(s32[16]{0:T(128)S(1)} %get-tuple-element.12.refs_9_) | copy-start | bytes 196

commit v9 on v8

--- a/solution.py
+++ b/solution.py
@@ -420,9 +420,10 @@
 
     load(5).wait()
     load(6).wait()
+    out_gens[0].drain()
+    out_gens[1].start()
     take_slots(0)
     gather_own(0)
-    out_gens[1].start()
     loop(0, 2, cotangent_tile)
     gather_next(0)
     take_slots(1)
@@ -461,7 +462,15 @@
     from_peer = [r.qkv.at[:, pl.ds(2048 + half * 512, 512)] for half in range(HALVES)]
     ring_z = [Ring(mine[half], r.ring_z[half][0], r.ring_z[half][1], "z", where, at) for half in range(HALVES)]
 
-    loop(0, 8, lambda b: attention_forward(b, r, mixed))
+    def forward_two(i):
+        attention_forward(i * 2, r, mixed)
+        attention_forward(i * 2 + 1, r, mixed)
+
+    def backward_two(i):
+        attention_backward(i * 2, r)
+        attention_backward(i * 2 + 1, r)
+
+    loop(0, 4, forward_two)
     mixed_t[...] = mixed[...].T
 
     def out_terms(i):
@@ -483,7 +492,7 @@
     loop(1, 4, out_terms)
     ring_oa.second()
     ring_ob.second()
-    loop(0, 8, lambda b: attention_backward(b, r))
+    loop(0, 4, backward_two)
 
     core_copies = [
         [
@@ -550,7 +559,8 @@
 
     def start_back_gen(half):
         ring_z[half].last(r.piece[half], 0, 16)
-        out_gens[half].drain()
+        if half == 1:
+            out_gens[half].drain()
         for j in range(32):
             r.outgoing[half][j] = r.piece[half][r.position[j]]
         back_gens[half].start()

time: 125 us -> 123 us (0.984)
  Pallas kernels: 121 us -> 119 us
    pallas_call x1, Pallas kernels: 118 us -> 117 us  [whole(): pl.pallas_call(functools.partial(whole_kernel, tree), name='retro_whole',...]
where the time goes in v9:
time: 123 us
  Pallas kernels  119 us (97%)
  other arithmetic  2.44 us (2%)
    pallas_call x1, Pallas kernels, whole(): pl.pallas_call(functools.partial(whole_kernel, tree), name='retro_whole',...  117 us

profile of v9, /device:TPU:1, one launch (start us, length us, event | category | flops | bytes accessed | tf_op | source)
XLA Modules:
  0.0 123.2 jit_solution(2229535268042509366)
XLA Ops:
  0.7 0.8 copy.18
  1.5 0.1 reshape.218
  1.6 0.1 reshape.219
  1.7 0.4 convert_reduce_fusion
  2.2 0.1 select_reduce_fusion.3
  2.3 0.0 copy-start
  2.3 0.1 add.77
  2.4 0.6 select_reduce_fusion.refs_10_
  3.0 0.6 select_reduce_fusion.1.refs_0_
  3.6 0.6 select_reduce_fusion.2.refs_7_
  4.2 0.0 copy-done
  4.2 116.6 %retro_whole.1 = (bf16[2,128,1024]{2,1,0:T(8,128)(2,1)}, bf16[64,512]{1,0:T(8,128)(2,1)}, bf16[512,256]{1,0:T(8,128)(2,1)}, bf16[64,512]{1,0:T(8,128)(2,1)}) custom-call(s32[16]{0:T(128)} %select_reduce_fusion.1.refs_0_, bf16[512,4096]{1,0:T(8,128)(2,1)} %refs_1_.1, f32[1,1024]{1,0:T(1,128)} %bitcast.5, bf16[1024,1024]{1,0:T(8,128)(2,1)} %refs_3_.1, ...), custom_call_target="tpu_custom_call" | custom-call | tf_op jit(solution)/shard_map/retro_whole/pallas_call | solution.py:706
  120.8 2.4 %widen.1 = (f32[2,128,1024]{2,1,0:T(8,128)}, f32[512,256]{1,0:T(8,128)}, f32[64,512]{1,0:T(8,128)}, f32[64,512]{1,0:T(8,128)}) custom-call(bf16[2,128,1024]{2,1,0:T(8,128)(2,1)} %get-tuple-element.8.refs_0_, bf16[512,256]{1,0:T(8,128)(2,1)} %get-tuple-element.9.refs_1_, bf16[64,512]{1,0:T(8,128)(2,1)} %get-tuple-element.10.refs_2_, ...), custom_call_target="tpu_custom_call" | custom-call | tf_op jit(solution)/shard_map/widen/pallas_call | solution.py:732
  (6 shorter events, 0.1 us)
Async XLA Ops:
  2.3 2.0 %copy-start = (s32[16]{0:T(128)}, s32[16]{0:T(128)S(1)}, u32[]{:S(2)}) copy-start(s32[16]{0:T(128)S(1)} %get-tuple-element.12.refs_9_) | copy-start | bytes 196
